TPU v7x, 32 devices: a whole 2x2x4 slice. The times are simulated.
32 devices in a mesh: gz: 2 (over x), gx: 4 (over y, core), gy: 4 (over z).
Axes of the slice: x: 2, y: 2, z: 4, core: 2. Of those that a mesh axis runs over, the one named last changes fastest.
Arguments:
- sections: bfloat16 [2, 2560, 2560], P('gz', 'gy', 'gx'), may hold values from -440 to 440
- peaks: int32 [2, 2, 40, 40], P('gz', None, 'gy', 'gx'), may hold values from 0 to 127
- valid: int32 [2, 40, 40], P('gz', 'gy', 'gx'), may hold values 0 or 1
Outputs:
- fit: float32 [2, 6, 40, 40], P('gz', None, 'gy', 'gx')
All inputs are finite; a program needn't handle non-finite values. Where the computation divides by a largest or mean magnitude, that divisor is 1e-20 or more. No bound on the sum of `valid` on one device may be relied on, other than what follows from the above.
Results may differ from a plain program's by a relative error of at most 0.0089.
Values may be sent and summed in bfloat16 or wider, within the bound.
No kernel may reach another device: no remote copies, remote signals or barrier semaphores. Data moves between devices by JAX's collectives and lax.ppermute only.
A program may use at most 64 MiB of HBM per device.

v0:
```python
import functools
import math

import jax
import jax.numpy as jnp
import numpy as np
from jax import lax
from jax.experimental import pallas as pl
from jax.experimental.pallas import tpu as pltpu
from jax.sharding import PartitionSpec as P


PATCH = 128
STRIDE = 64
WIN = 5
HALF = PATCH // 2
EDGE = 8
SLOT = 16
PARTS = 2
F32 = jnp.float32
BF16 = jnp.bfloat16


def tables():
    index = np.arange(PATCH)
    phase = (index[:, None] * index[None, :] % PATCH).astype(np.float64) * (2.0 * math.pi / PATCH)
    cosine = np.asarray(np.cos(phase), dtype=jnp.bfloat16).astype(np.float32)
    sine = np.asarray(np.sin(phase), dtype=jnp.bfloat16).astype(np.float32)
    first = np.zeros((4 * HALF, 2 * PATCH), np.float32)
    for part, table in enumerate((cosine, -sine)):
        for which in range(2):
            top = part * PATCH + which * HALF
            first[top : top + HALF, which * STRIDE : which * STRIDE + PATCH] = table[:HALF]
    second = np.block([[cosine, -sine], [sine, cosine]])
    third = np.block([[cosine, sine], [-sine, cosine]])
    weight = np.where(np.arange(HALF) == 0, 1.0, 2.0)[None, :]
    fourth = np.concatenate(
        [cosine[:, :HALF] * weight, -sine[:, :HALF] * weight, np.repeat(cosine[:, HALF : HALF + 1], SLOT, 1)], 1
    )
    return first, second, third, fourth, cosine[HALF]


def middle_rows(middle, pairs):
    rows = np.zeros((pairs, SLOT, 2 * PATCH), np.float32)
    for pair in range(pairs):
        for which in range(2):
            rows[pair, 2 * pair + which, which * STRIDE : which * STRIDE + PATCH] = middle
    return rows


def columns_mask(blocks, columns):
    mask = np.zeros((blocks * PATCH, PATCH), np.float32)
    for column in range(columns):
        mask[column * STRIDE : column * STRIDE + PATCH, column] = 1.0
    return mask


class Tables:
    def __init__(self, ref, pairs):
        self.ref, self.pairs = ref, pairs

    def rows(self, top, count):
        return self.ref[top : top + count, :]

    def first(self):
        return self.rows(0, 2 * PATCH)

    def middle(self, pair):
        return self.rows(6 * PATCH + PATCH + pair * SLOT, SLOT)

    def second(self):
        return self.rows(2 * PATCH, 2 * PATCH)

    def third(self):
        return self.rows(4 * PATCH, 2 * PATCH)

    def fourth(self):
        return self.ref[6 * PATCH : 7 * PATCH, : PATCH + SLOT]

    def mask(self):
        value = self.rows(7 * PATCH + self.pairs * SLOT, (self.pairs + 1) * PATCH // 2)
        return jnp.concatenate([value[:, :PATCH], value[:, PATCH:]], 0)


def all_tables(blocks, columns):
    first, second, third, fourth, middle = tables()
    fourth = np.pad(fourth, ((0, 0), (0, 2 * PATCH - fourth.shape[1])))
    mask = columns_mask(blocks, columns)
    half = mask.shape[0] // 2
    return np.concatenate(
        [
            first, second, third, fourth, middle_rows(middle, columns // 2).reshape(-1, 2 * PATCH),
            np.concatenate([mask[:half], mask[half:]], 1),
        ],
        0,
    )


def passed_along(value, axis, steps):
    count = lax.axis_size(axis)
    initial, last = (max(0, -steps), min(count, count - steps))
    return lax.ppermute(value, axis, [(source, source + steps) for source in range(initial, last)])


def side_by_side(value):
    rows = value.shape[0] // 2
    return jnp.concatenate([value[:rows, :STRIDE], value[rows:, :STRIDE]], 1)


def two_terms(value):
    high = value.astype(BF16)
    return high, (value - high.astype(F32)).astype(BF16)


def only_low(value):
    low = lax.broadcasted_iota(jnp.int32, value.shape, 1) < STRIDE
    return jnp.where(low, value.astype(F32), 0.0).astype(BF16)


def parts(rows, first=0):
    step = (rows - first) // PARTS
    return [slice(top, top + step) for top in range(first, rows, step)]


def window_of(chunk, start, block):
    return jnp.concatenate([chunk(start, block), chunk(start + 1, block)], 0)


def forward(chunk, start, table, columns_of, chosen=None):
    pairs = table.pairs
    total = jnp.zeros((SLOT, 2 * PATCH), F32)
    for pair in range(pairs) if chosen is None else chosen:
        right = jnp.concatenate(
            [
                jnp.concatenate([window_of(chunk, start + w, pair + half) for half in range(2)], 1)
                for w in range(2)
            ],
            0,
        )
        left = jnp.concatenate([table.first(), table.middle(pair)], 0)
        out = lax.dot_general(left, right, (((1,), (1,)), ((), ())), preferred_element_type=F32)
        one = out[: 2 * PATCH].astype(BF16)
        for w in range(2):
            top = (2 * pair + w) * PATCH
            columns_of[top : top + PATCH, :PATCH] = one[:PATCH, w * PATCH : (w + 1) * PATCH]
            columns_of[top : top + PATCH, PATCH:] = one[PATCH:, w * PATCH : (w + 1) * PATCH]
        total += out[2 * PATCH :]
    value = total.astype(BF16)
    top = 2 * pairs * PATCH
    for w in range(2):
        columns_of[top + w * SLOT : top + (w + 1) * SLOT, :PATCH] = value[:, w * PATCH : (w + 1) * PATCH]
    columns_of[top : top + 2 * SLOT, PATCH:] = jnp.zeros((2 * SLOT, PATCH), BF16)


def energies(chunk, blocks, first_row, patch_rows, mask, sums):
    for row in range(patch_rows + 1):
        for block in range(blocks):
            pixels = chunk(first_row + row, block).astype(F32)
            sums[row : row + 1, block * PATCH : (block + 1) * PATCH] = jnp.sum(pixels * pixels, axis=0, keepdims=True)
    both = sums[0:patch_rows, :] + sums[1 : patch_rows + 1, :]
    total = sum(jnp.dot(term, mask, preferred_element_type=F32) for term in two_terms(both))
    return total * (1.0 / (PATCH * PATCH))


def prepare_kernel(upper_rows, merged, active, tile, peaks, constants, *refs):
    rows, columns = tile.shape
    patch_rows = rows // STRIDE
    height = (upper_rows + 1) * STRIDE
    first_lower = upper_rows * STRIDE
    lower = rows - first_lower
    sends = 2 if merged else 4
    outs, (whole, top, left, held), (numbers, packed, sems) = refs[:sends], refs[sends : sends + 4], refs[sends + 4 :]
    wide = columns - PATCH
    blocks = columns // PATCH

    def upwards(early, late, sem):
        return [
            pltpu.make_async_copy(tile.at[:height, :PATCH], early, sems.at[sem]),
            pltpu.make_async_copy(tile.at[:height, PATCH:], late, sems.at[sem + 1]),
        ]

    def downwards(early, late, sem):
        copies = [
            (tile.at[:STRIDE, block * PATCH : (block + 1) * PATCH], early.at[block * STRIDE : (block + 1) * STRIDE, :])
            for block in range(blocks)
        ]
        copies.append((tile.at[first_lower:, :wide], late.at[:lower, :]))
        for half in range(2):
            start = first_lower + half * lower // 2
            copies.append(
                (
                    tile.at[start : start + lower // 2, wide:],
                    late.at[lower : lower + lower // 2, half * PATCH : (half + 1) * PATCH],
                )
            )
        return [pltpu.make_async_copy(a, b, sems.at[sem + k]) for k, (a, b) in enumerate(copies)]

    def add_peaks(late):
        packed[...] = jnp.zeros_like(packed)
        for i in range(patch_rows - upper_rows):
            packed[2 * i : 2 * i + 2, : peaks.shape[2]] = numbers[upper_rows + i].astype(F32)
        late[lower + lower // 2 : lower + lower // 2 + SLOT, :PATCH] = packed[...].astype(BF16)

    fixed = [
        pltpu.make_async_copy(peaks, numbers, sems.at[0]),
        pltpu.make_async_copy(tile, whole, sems.at[1]),
        pltpu.make_async_copy(tile.at[:STRIDE, :], top, sems.at[2]),
        pltpu.make_async_copy(tile.at[:, :PATCH], left, sems.at[3]),
        pltpu.make_async_copy(constants, held, sems.at[4]),
    ]
    ups = upwards(outs[0], outs[1], 5)
    downs = downwards(outs[-2], outs[-1], 7)

    def start(copies):
        for copy in copies:
            copy.start()

    def wait(copies):
        for copy in copies:
            copy.wait()

    if merged:
        pl.when(active[1] > 0)(lambda: start(ups))
        pl.when(active[1] == 0)(lambda: start(downs))
    else:
        start(ups)
        start(downs)
    start(fixed)
    fixed[0].wait()
    if merged:
        pl.when(active[1] == 0)(lambda: add_peaks(outs[-1]))
        pl.when(active[1] > 0)(lambda: wait(ups))
        pl.when(active[1] == 0)(lambda: wait(downs))
    else:
        add_peaks(outs[-1])
        wait(ups)
        wait(downs)
    wait(fixed[1:])


def own_inner_kernel(upper_rows, active, tile, constants, spectra, once):
    rows, columns = tile.shape
    patch_rows = rows // STRIDE
    blocks = columns // PATCH
    table = Tables(constants, blocks)

    def chunk(row, block):
        return tile[row * STRIDE : (row + 1) * STRIDE, block * PATCH : (block + 1) * PATCH]

    inner = 2 * (blocks - 1) * PATCH
    for slot, (lowest, highest) in enumerate(((0, upper_rows), (upper_rows, patch_rows - 2))):

        @pl.when(active[slot] > 0)
        def _(lowest=lowest, highest=highest):
            for step in range(lowest // 2, highest // 2):
                columns_of = once.at[step % 2]
                forward(chunk, 2 * step, table, columns_of, range(blocks - 1))
                depth = columns_of.shape[0]
                for part in parts(inner) + [slice(depth - 2 * SLOT, depth)]:
                    value = jnp.dot(columns_of[part, :], table.second(), preferred_element_type=F32)
                    spectra[step, part, :] = value.astype(BF16)


def own_rest_kernel(
    upper_rows, active, tile, below, beside, constants, started, spectra, energy, strip, sums, once
):
    rows, columns = tile.shape
    patch_rows = rows // STRIDE
    blocks = columns // PATCH
    table = Tables(constants, blocks)
    strip[...] = only_low(beside[...])

    def chunk(row, block):
        at = slice(row * STRIDE, (row + 1) * STRIDE)
        if block == blocks:
            return strip[at, :]
        lanes = slice(block * PATCH, (block + 1) * PATCH)
        return tile[at, lanes] if row < patch_rows else below[:, lanes]

    inner = 2 * (blocks - 1) * PATCH
    for slot, (lowest, highest) in enumerate(((0, upper_rows), (upper_rows, patch_rows))):

        @pl.when(active[slot] > 0)
        def _(slot=slot, lowest=lowest, highest=highest):
            for step in range(lowest // 2, highest // 2):
                columns_of = once.at[step % 2]
                depth = columns_of.shape[0]
                last = step == patch_rows // 2 - 1
                forward(chunk, 2 * step, table, columns_of, None if last else [blocks - 1])
                for part in parts(depth, 0 if last else inner):
                    value = jnp.dot(columns_of[part, :], table.second(), preferred_element_type=F32)
                    middle = max(part.start, depth - 2 * SLOT)
                    if last or part.stop <= middle:
                        spectra[step, part, :] = value.astype(BF16)
                    else:
                        size = part.stop - middle
                        spectra[step, part.start : middle, :] = value[:-size].astype(BF16)
                        before = spectra[step, middle : part.stop, :].astype(F32)
                        spectra[step, middle : part.stop, :] = (before + value[-size:]).astype(BF16)
            energy[slot, : highest - lowest, :] = energies(
                chunk, blocks + 1, lowest, highest - lowest, table.mask(), sums
            )


def crossed(own, other, flipped):
    own = own.astype(F32)
    own_re, own_im = own[:, :PATCH], own[:, PATCH:]
    re, im = other[:, :PATCH], other[:, PATCH:]
    real = own_re * re + own_im * im
    imaginary = own_im * re - own_re * im if flipped else own_re * im - own_im * re
    return jnp.concatenate([real.astype(BF16), imaginary.astype(BF16)], 1)


def pair_kernel(
    slot, first_row, patch_rows, patch_columns, active, peaks, early, late, beside, spectra, energy,
    constants, out, strip, sums, once, crosses, inverse, peak, moments, offsets,
    *surfaces
):
    flipped = slot == 1
    size = patch_rows * SLOT
    pairs = patch_columns // 2
    blocks = pairs
    table = Tables(constants, pairs)

    @pl.when(active[slot] == 0)
    def _():
        out[...] = jnp.zeros_like(out)

    @pl.when(active[slot] > 0)
    def _():
        if flipped:
            half = strip.shape[0] // 2
            packed = beside[...].astype(F32)
            low = lax.broadcasted_iota(jnp.int32, packed.shape, 1) < STRIDE
            strip[:half, :] = jnp.where(low, packed, 0.0).astype(BF16)
            strip[half:, :] = jnp.where(low, pltpu.roll(packed, STRIDE, 1), 0.0).astype(BF16)
        else:
            packed = beside[: strip.shape[0], :].astype(F32)
            strip[...] = only_low(pltpu.roll(packed, STRIDE, 1))

        def chunk(row, block):
            at = slice(row * STRIDE, (row + 1) * STRIDE)
            if block == blocks:
                return strip[at, :]
            if not flipped:
                return early[at, :] if block == 0 else late[at, (block - 1) * PATCH : block * PATCH]
            if row == patch_rows:
                return early[block * STRIDE : (block + 1) * STRIDE, :]
            if block < blocks - 1:
                return late[at, block * PATCH : (block + 1) * PATCH]
            side, place = divmod(row, patch_rows // 2)
            top = (patch_rows + place) * STRIDE
            return late[top : top + STRIDE, side * PATCH : (side + 1) * PATCH]

        row_of = lax.broadcasted_iota(jnp.int32, (SLOT, 2 * PATCH), 0)
        for step in range(patch_rows // 2):
            columns_of, cross, back = once.at[step % 2], crosses.at[step % 2], inverse.at[step % 2]
            forward(chunk, 2 * step, table, columns_of)
            for part in parts(columns_of.shape[0]):
                spectrum = jnp.dot(columns_of[part, :], table.second(), preferred_element_type=F32)
                cross[part, :] = crossed(spectra[step + first_row // 2, part, :], spectrum, flipped)
            for part in parts(columns_of.shape[0]):
                back[part, :] = jnp.dot(cross[part, :], table.third(), preferred_element_type=F32).astype(BF16)
            top = 2 * pairs * PATCH
            mid = back[top : top + 2 * SLOT, :PATCH].astype(F32)
            mid = jnp.concatenate([mid[:SLOT], mid[SLOT:]], 1)
            for column in range(patch_columns):
                a = (column // 2) * 2 * PATCH + (column % 2) * HALF
                b = a + PATCH
                right = jnp.concatenate(
                    [
                        jnp.concatenate([back[a : a + HALF, :PATCH], back[b : b + HALF, :PATCH]], 1),
                        jnp.concatenate([back[a : a + HALF, PATCH:], back[b : b + HALF, PATCH:]], 1),
                        jnp.where(row_of == column, mid, 0.0).astype(BF16),
                    ],
                    0,
                )
                value = jnp.dot(table.fourth(), right, preferred_element_type=F32)
                largest = jnp.max(jnp.abs(value), axis=0, keepdims=True)
                for which in range(2):
                    lanes = slice(which * PATCH, (which + 1) * PATCH)
                    i = 2 * step + which
                    at = i * SLOT + column
                    surface = surfaces[2 * column + which]
                    surface[EDGE : EDGE + PATCH, :] = value[:, lanes]
                    surface[:EDGE, :] = value[PATCH - EDGE :, lanes]
                    surface[EDGE + PATCH :, :] = value[:EDGE, lanes]
                    peak[at : at + 1, :] = largest[:, lanes]
                    along = peaks[i, 1, column] + (EDGE - WIN // 2)
                    moments[at * 8 : at * 8 + 8, :] = surface[pl.ds(along, 8), :]
                    offsets[at : at + 1, :] = jnp.full((1, PATCH), peaks[i, 0, column], jnp.int32)
        other = energies(chunk, blocks + 1, 0, patch_rows, table.mask(), sums)
        scales = float(PATCH) ** 3 * jnp.sqrt((energy[slot, :patch_rows, :] + 1e-05) * (other + 1e-05))

        lane = lax.broadcasted_iota(jnp.int32, (1, PATCH), 1)
        scale = jnp.ones((1, PATCH), F32)
        for i in range(patch_rows):
            row = scales[i : i + 1, :]
            row = pltpu.roll(row, i * SLOT, 1) if i else row
            scale = jnp.where((lane >= i * SLOT) & (lane < i * SLOT + patch_columns), row, scale)
        peak_rows = peak[...]
        height = jnp.max(jnp.transpose(peak_rows), axis=0, keepdims=True) / scale + 1e-05

        lane = lax.broadcasted_iota(jnp.int32, (size, PATCH), 1)
        offset = (lane - offsets[...] + (WIN // 2 + PATCH)) & (PATCH - 1)
        u = (offset - WIN // 2).astype(F32)
        within = offset < WIN
        numbers = np.arange(WIN) - WIN // 2
        middle_square = float(np.mean(numbers**2))
        u0 = jnp.where(within, 1.0, 0.0)
        u1 = jnp.where(within, u, 0.0)
        u2 = jnp.where(within, u * u - middle_square, 0.0)
        v0 = v1 = v2 = jnp.zeros((size, PATCH), F32)
        for v in range(WIN):
            value = moments[pl.ds(v, size, stride=8), :]
            position = float(v - WIN // 2)
            v0 += value
            v1 += position * value
            v2 += (position * position - middle_square) * value
        factors = ((u0, v0), (u1, v0), (u0, v1), (u2, v0), (u0, v2), (u1, v1))
        terms = [two_terms(fu * fv) for fu, fv in factors]
        which_e = lax.broadcasted_iota(jnp.int32, (SLOT, len(terms) * PATCH), 0)
        of_lane = lax.broadcasted_iota(jnp.int32, (SLOT, len(terms) * PATCH), 1)
        ones = jnp.where((of_lane >= which_e * PATCH) & (of_lane < (which_e + 1) * PATCH), 1.0, 0.0).astype(BF16)
        total = sum(
            lax.dot_general(
                ones, jnp.concatenate([t[k] for t in terms], 1), (((1,), (1,)), ((), ())), preferred_element_type=F32
            )
            for k in range(2)
        )[:8]
        linear = float(np.sum(numbers**2))
        quadratic = float(np.sum((numbers**2 - middle_square) ** 2))
        norms = (
            float(WIN), math.sqrt(WIN * linear), math.sqrt(WIN * linear), math.sqrt(WIN * quadratic),
            math.sqrt(WIN * quadratic), linear,
        )
        e_row = lax.broadcasted_iota(jnp.int32, (8, size), 0)
        factor = jnp.zeros((8, size), F32)
        for e, norm in enumerate(norms):
            factor = jnp.where(e_row == e, 1.0 / norm, factor)
        out[:, :size] = total * factor / (scale * height)[:, :size]
        if size < PATCH:
            out[:, size:] = jnp.zeros((8, PATCH - size), F32)


def join_kernel(upper_rows, upper, lower, valid, out):
    count, patch_rows, _, patch_columns = out.shape
    for i in range(patch_rows):
        source, at = (upper, i) if i < upper_rows else (lower, i - upper_rows)
        value = source[...]
        turned = pltpu.roll(value, PATCH - at * SLOT, 1) if at else value
        keep = valid[i].astype(F32)
        for e in range(count):
            out[e, i] = turned[e : e + 1, :patch_columns] * keep


def body(sections, peaks, valid):
    tile = sections[0]
    rows, columns = tile.shape
    patch_rows, patch_columns = rows // STRIDE, columns // STRIDE
    pairs = patch_columns // 2
    upper_rows = (patch_rows // 2 + 1) // 2 * 2
    lower_rows = patch_rows - upper_rows
    first_lower = upper_rows * STRIDE
    upper_height = first_lower + STRIDE
    lower_height = lower_rows * STRIDE + STRIDE
    count, height = lax.axis_size("gz"), lax.axis_size("gy")
    position = lax.axis_index("gz")
    active = jnp.stack([position < count - 1, position > 0]).astype(jnp.int32)
    peaks = jnp.transpose(peaks, (0, 2, 1, 3))[0]
    valid = jnp.transpose(valid, (1, 0, 2))

    constants = jnp.asarray(all_tables(columns // PATCH + 1, patch_columns), BF16)

    vmem = pl.BlockSpec(memory_space=pltpu.VMEM)
    smem = pl.BlockSpec(memory_space=pltpu.SMEM)

    def grant(mib):
        return pltpu.CompilerParams(vmem_limit_bytes=mib << 20)

    def shape(*dims, dtype=BF16):
        return jax.ShapeDtypeStruct(dims, dtype)

    merged = count == 2
    early, late = shape(upper_height, PATCH), shape(upper_height, columns - PATCH)
    anywhere = pl.BlockSpec(memory_space=pltpu.HBM)
    outs = pl.pallas_call(
        functools.partial(prepare_kernel, upper_rows, merged),
        out_shape=((early, late) if merged else (early, late) * 2)
        + (shape(rows, columns), shape(STRIDE, columns), shape(rows, PATCH), shape(*constants.shape)),
        in_specs=[smem] + [anywhere] * 3,
        out_specs=(vmem,) * (6 if merged else 8),
        scratch_shapes=[
            pltpu.VMEM(peaks.shape, jnp.int32),
            pltpu.VMEM((SLOT, PATCH), F32),
            pltpu.SemaphoreType.DMA((7 + columns // PATCH + 3,)),
        ],
        compiler_params=grant(1),
        name="prepare",
    )(active, *(pltpu.with_memory_space_constraint(x, pltpu.HBM) for x in (tile, peaks, constants)))
    tile, top, left, constants = outs[-4:]

    up = [((s + 1) * height + y, s * height + y) for s in range(count - 1) for y in range(height)]
    down = [(s * height + y + 1, (s + 1) * height + y) for s in range(count - 1) for y in range(height - 1)]
    if merged:
        early_upper = early_lower = lax.ppermute(outs[0], ("gz", "gy"), up + down)
        late_upper = late_lower = lax.ppermute(outs[1], "gz", [(0, 1), (1, 0)])
    else:
        early_upper = lax.ppermute(outs[0], ("gz", "gy"), up)
        early_lower = lax.ppermute(outs[2], ("gz", "gy"), down)
        late_upper = passed_along(outs[1], "gz", -1)
        late_lower = passed_along(outs[3], "gz", 1)
    below = passed_along(top, "gy", -1)
    others = jnp.pad(early_upper[:, :STRIDE], ((0, rows + STRIDE - upper_height), (0, 0)))
    ours = jnp.concatenate([left[:, :STRIDE], below[:, :STRIDE]], 0)
    beside = passed_along(jnp.concatenate([ours, others], 1), "gx", -1)
    edge_lower = passed_along(side_by_side(beside[first_lower : rows + STRIDE]), "gz", 1)

    steps = patch_rows // 2
    depth = 2 * pairs * PATCH + 2 * SLOT
    width = columns + PATCH
    own_cost = pl.CostEstimate(flops=2_000_000_000, bytes_accessed=6_000_000, transcendentals=0)
    own_inner = pl.pallas_call(
        functools.partial(own_inner_kernel, upper_rows),
        out_shape=shape(steps, depth, 2 * PATCH),
        in_specs=[smem] + [vmem] * 2,
        out_specs=vmem,
        scratch_shapes=[pltpu.VMEM((2, depth, 2 * PATCH), BF16)],
        compiler_params=grant(6),
        cost_estimate=own_cost,
        name="own_inner",
    )
    spectra = own_inner(active, tile, constants)
    own_rest = pl.pallas_call(
        functools.partial(own_rest_kernel, upper_rows),
        out_shape=(shape(steps, depth, 2 * PATCH), shape(2, 8, PATCH, dtype=F32)),
        in_specs=[smem] + [vmem] * 5,
        out_specs=(vmem, vmem),
        scratch_shapes=[
            pltpu.VMEM((rows + STRIDE, PATCH), BF16),
            pltpu.VMEM((8, width), F32),
            pltpu.VMEM((2, depth, 2 * PATCH), BF16),
        ],
        input_output_aliases={5: 0},
        compiler_params=grant(6),
        cost_estimate=own_cost,
        name="own_rest",
    )
    spectra, energy = own_rest(active, tile, below, beside, constants, spectra)

    def correlated(slot, first_row, count_rows, strip_rows, peaks_here, early, late, beside):
        size = count_rows * SLOT
        return pl.pallas_call(
            functools.partial(pair_kernel, slot, first_row, count_rows, patch_columns),
            out_shape=shape(8, PATCH, dtype=F32),
            in_specs=[smem, smem] + [vmem] * 6,
            out_specs=vmem,
            scratch_shapes=[
                pltpu.VMEM((strip_rows, PATCH), BF16),
                pltpu.VMEM((8, width), F32),
                pltpu.VMEM((2, depth, 2 * PATCH), BF16),
                pltpu.VMEM((2, depth, 2 * PATCH), BF16),
                pltpu.VMEM((2, depth, 2 * PATCH), BF16),
                pltpu.VMEM((PATCH, PATCH), F32),
                pltpu.VMEM((size * 8, PATCH), F32),
                pltpu.VMEM((size, PATCH), jnp.int32),
            ]
            + [pltpu.VMEM((PATCH + 2 * EDGE, PATCH), F32)] * (2 * patch_columns),
            compiler_params=grant(12),
            cost_estimate=pl.CostEstimate(flops=4_000_000_000, bytes_accessed=6_000_000, transcendentals=0),
        )(active, peaks_here, early, late, beside, spectra, energy, constants)

    at = lower_rows * STRIDE + lower_rows * STRIDE // 2
    peaks_lower = late_lower[at : at + 2 * lower_rows, :patch_columns].astype(jnp.int32)
    peaks_lower = peaks_lower.reshape(lower_rows, 2, patch_columns)
    lower = correlated(1, upper_rows, lower_rows, lower_height, peaks_lower, early_lower, late_lower, edge_lower)
    lower = passed_along(lower, "gz", -1)
    upper = correlated(0, 0, upper_rows, upper_height, peaks, early_upper, late_upper, beside)
    fit = pl.pallas_call(
        functools.partial(join_kernel, upper_rows),
        out_shape=shape(6, patch_rows, 1, patch_columns, dtype=F32),
        in_specs=[vmem] * 3,
        out_specs=vmem,
        compiler_params=grant(1),
        name="join",
    )(upper, lower, valid)
    return jnp.transpose(fit, (2, 0, 1, 3))


def solution(mesh):
    in_specs = (P("gz", "gy", "gx"), P("gz", None, "gy", "gx"), P("gz", "gy", "gx"))
    out_specs = P("gz", None, "gy", "gx")
    return jax.shard_map(body, mesh=mesh, in_specs=in_specs, out_specs=out_specs, check_vma=False)
```

profile of v0, /device:TPU:1, one launch (start us, length us, event | category | flops | bytes accessed | tf_op | source)
XLA Modules:
  0.0 31.7 jit_solution(14644755195518307230)
XLA Ops:
  0.0 0.1 add_convert_fusion.active
  0.1 2.3 %prepare.1 = (bf16[448,128]{1,0:T(8,128)(2,1)S(1)}, bf16[448,512]{1,0:T(8,128)(2,1)S(1)}, bf16[640,640]{1,0:T(8,128)(2,1)S(1)}, bf16[64,640]{1,0:T(8,128)(2,1)S(...) custom-call(s32[2]{0:T(128)S(1)} %add_convert_fusion.active, bf16[640,640]{1,0:T(8,128)(2,1)} %bitcast.17, ...), custom_call_target="tpu_custom_call" | custom-call | tf_op jit(solution)/shard_map/prepare/pallas_call | solution.py:487
  2.4 1.3 %collective-permute-start = (bf16[448,128]{1,0:T(8,128)(2,1)S(1)}, bf16[448,128]{1,0:T(8,128)(2,1)S(1)}, u32[]{:S(2)}, u32[]{:S(2)}) collective-permute-start(bf16[448,128]{1,0:T(8,128)(2,1)S(1)} %get-tuple-element.13), channel_id=1, source_target_pairs={{16,0},{17,1},{18,2},{19,3},{1,16},{2,17},{3,18},{20,4},{21,5},{22... | collective-permute-start | bytes 344072 | tf_op jit(solution)/shard_map/ppermute | solution.py:506
  3.7 1.3 %collective-permute-start.2 = (bf16[64,640]{1,0:T(8,128)(2,1)S(1)}, bf16[64,640]{1,0:T(8,128)(2,1)S(1)}, u32[]{:S(2)}, u32[]{:S(2)}) collective-permute-start(bf16[64,640]{1,0:T(8,128)(2,1)S(1)} %get-tuple-element.16), channel_id=1, source_target_pairs={{1,0},{2,1},{3,2},{5,4},{6,5},{7,6},{9,8},{10,9},{11,10},{13,12},{... | collective-permute-start | bytes 245768 | tf_op jit(solution)/shard_map/ppermute | solution.py:102
  5.0 2.7 %collective-permute-start.1 = (bf16[448,512]{1,0:T(8,128)(2,1)S(1)}, bf16[448,512]{1,0:T(8,128)(2,1)S(1)}, u32[]{:S(2)}, u32[]{:S(2)}) collective-permute-start(bf16[448,512]{1,0:T(8,128)(2,1)S(1)} %get-tuple-element.14), channel_id=1, source_target_pairs={{0,16},{16,0},{1,17},{17,1},{2,18},{18,2},{3,19},{19,3},{4,20},{20... | collective-permute-start | bytes 1376264 | tf_op jit(solution)/shard_map/ppermute | solution.py:507
  7.7 4.6 %collective-permute-done.2.below = bf16[64,640]{1,0:T(8,128)(2,1)S(1)} collective-permute-done((bf16[64,640]{1,0:T(8,128)(2,1)S(1)}, bf16[64,640]{1,0:T(8,128)(2,1)S(1)}, u32[]{:S(2)}, u32[]{:S(2)}) %collective-permute-start.2) | collective-permute-done | bytes 81952 | tf_op jit(solution)/shard_map/ppermute | solution.py:102
  12.4 0.0 collective-permute-done.early
  12.4 0.1 fusion.1
  12.5 2.9 %collective-permute-start.3 = (bf16[704,128]{1,0:T(8,128)(2,1)S(1)}, bf16[704,128]{1,0:T(8,128)(2,1)S(1)}, u32[]{:S(2)}, u32[]{:S(2)}) collective-permute-start(bf16[704,128]{1,0:T(8,128)(2,1)S(1)} %fusion.1), channel_id=1, source_target_pairs={{4,0},{8,4},{12,8},{5,1},{9,5},{13,9},{6,2},{10,6},{14,10},{7,3},{... | collective-permute-start | bytes 540680 | tf_op jit(solution)/shard_map/ppermute | solution.py:102
  15.4 1.9 %own_inner.1.started = bf16[5,1312,256]{2,1,0:T(8,128)(2,1)S(1)} custom-call(s32[2]{0:T(128)S(1)} %add_convert_fusion.active, bf16[640,640]{1,0:T(8,128)(2,1)S(1)} %get-tuple-element.17.tile, bf16[1360,256]{1,0:T(8,128)(2,1)S(1)} %get-tuple-element.18.constants), custom_call_target="tpu_custom_call" | custom-call | flops 2000000000 | bytes 6000000 | tf_op jit(solution)/shard_map/own_inner/pallas_call | solution.py:533
  17.3 2.6 %collective-permute-done.3.beside = bf16[704,128]{1,0:T(8,128)(2,1)S(1)} collective-permute-done((bf16[704,128]{1,0:T(8,128)(2,1)S(1)}, bf16[704,128]{1,0:T(8,128)(2,1)S(1)}, u32[]{:S(2)}, u32[]{:S(2)}) %collective-permute-start.3) | collective-permute-done | bytes 180256 | tf_op jit(solution)/shard_map/ppermute | solution.py:102
  19.9 0.1 pad_maximum_fusion
  20.0 2.5 %collective-permute-start.4 = (bf16[160,128]{1,0:T(8,128)(2,1)S(1)}, bf16[160,128]{1,0:T(8,128)(2,1)S(1)}, u32[]{:S(2)}, u32[]{:S(2)}) collective-permute-start(bf16[160,128]{1,0:T(8,128)(2,1)S(1)} %pad_maximum_fusion), channel_id=1, source_target_pairs={{0,16},{1,17},{2,18},{3,19},{4,20},{5,21},{6,22},{7,23},{8,24},{9,... | collective-permute-start | bytes 122888 | tf_op jit(solution)/shard_map/ppermute | solution.py:102
  22.5 1.3 %own_rest.1 = (bf16[5,1312,256]{2,1,0:T(8,128)(2,1)S(1)}, f32[2,8,128]{2,1,0:T(8,128)S(1)}) custom-call(s32[2]{0:T(128)S(1)} %add_convert_fusion.active, bf16[640,640]{1,0:T(8,128)(2,1)S(1)} %get-tuple-element.17.tile, bf16[64,640]{1,0:T(8,128)(2,1)S(1)} %collective-permute-done.2.below, ...), custom_call_target="tpu_custom_call", output_to_operand_aliasing={{0}: (5, {})} | custom-call | flops 2000000000 | bytes 6000000 | tf_op jit(solution)/shard_map/own_rest/pallas_call | solution.py:549
  23.8 0.0 collective-permute-done.1.late
  23.8 0.0 collective-permute-done.4.beside
  23.9 0.0 copy-start
  23.9 0.6 %shard_map.47 = f32[8,128]{1,0:T(8,128)S(1)} custom-call(s32[2]{0:T(128)S(1)} %add_convert_fusion.active, s32[4,2,10]{2,1,0:T(2,128)S(1)} %convert.1.peaks, bf16[448,128]{1,0:T(8,128)(2,1)S(1)} %collective-permute-done.early, bf16[448,512]{1,0:T(8,128)(2,1)S(1)} %collective-permute-done.1.late, bf16[160,128]{1,0:T(8,128)(2,1)S(1)} %collective-permute-done.4.beside, ...), custom_call_target="tpu_custom_call" | custom-call | flops 4000000000 | bytes 6000000 | tf_op jit(solution)/shard_map/pallas_call | solution.py:553
  24.5 0.0 copy-start.1
  24.5 1.3 %collective-permute-start.5 = (f32[8,128]{1,0:T(8,128)S(1)}, f32[8,128]{1,0:T(8,128)S(1)}, u32[]{:S(2)}, u32[]{:S(2)}) collective-permute-start(f32[8,128]{1,0:T(8,128)S(1)} %shard_map.47), channel_id=1, source_target_pairs={{16,0},{17,1},{18,2},{19,3},{20,4},{21,5},{22,6},{23,7},{24,8},{25... | collective-permute-start | bytes 12296 | tf_op jit(solution)/shard_map/ppermute | solution.py:102
  25.8 0.0 copy-done
  25.8 4.4 %shard_map.46.upper = f32[8,128]{1,0:T(8,128)S(1)} custom-call(s32[2]{0:T(128)S(1)} %add_convert_fusion.active, s32[10,2,10]{2,1,0:T(2,128)S(1)} %bitcast.15, bf16[448,128]{1,0:T(8,128)(2,1)S(1)} %collective-permute-done.early, bf16[448,512]{1,0:T(8,128)(2,1)S(1)} %collective-permute-done.1.late, bf16[704,128]{1,0:T(8,128)(2,1)S(1)} %collective-permute-done.3.beside, ...), custom_call_target="tpu_custom_call" | custom-call | flops 4000000000 | bytes 6000000 | tf_op jit(solution)/shard_map/pallas_call | solution.py:553
  30.3 0.7 %collective-permute-done.5.lower = f32[8,128]{1,0:T(8,128)S(1)} collective-permute-done((f32[8,128]{1,0:T(8,128)S(1)}, f32[8,128]{1,0:T(8,128)S(1)}, u32[]{:S(2)}, u32[]{:S(2)}) %collective-permute-start.5) | collective-permute-done | bytes 4128 | tf_op jit(solution)/shard_map/ppermute | solution.py:102
  31.0 0.0 copy-done.1
  31.0 0.7 %join.1 = f32[6,10,1,10]{3,2,1,0:T(1,128)} custom-call(f32[8,128]{1,0:T(8,128)S(1)} %shard_map.46.upper, f32[8,128]{1,0:T(8,128)S(1)} %collective-permute-done.5.lower, s32[10,1,10]{2,1,0:T(1,128)S(1)} %bitcast.16), custom_call_target="tpu_custom_call" | custom-call | tf_op jit(solution)/shard_map/join/pallas_call | solution.py:579
  (4 shorter events, 0.0 us)
Async XLA Ops:
  2.4 10.0 %collective-permute-start = (bf16[448,128]{1,0:T(8,128)(2,1)S(1)}, bf16[448,128]{1,0:T(8,128)(2,1)S(1)}, u32[]{:S(2)}, u32[]{:S(2)}) collective-permute-start(bf16[448,128]{1,0:T(8,128)(2,1)S(1)} %get-tuple-element.13), channel_id=1, source_target_pairs={{16,0},{17,1},{18,2},{19,3},{1,16},{2,17},{3,18},{20,4},{21,5},{22... | collective-permute-start | bytes 344072 | tf_op jit(solution)/shard_map/ppermute | solution.py:506
  3.7 8.7 %collective-permute-start.2 = (bf16[64,640]{1,0:T(8,128)(2,1)S(1)}, bf16[64,640]{1,0:T(8,128)(2,1)S(1)}, u32[]{:S(2)}, u32[]{:S(2)}) collective-permute-start(bf16[64,640]{1,0:T(8,128)(2,1)S(1)} %get-tuple-element.16), channel_id=1, source_target_pairs={{1,0},{2,1},{3,2},{5,4},{6,5},{7,6},{9,8},{10,9},{11,10},{13,12},{... | collective-permute-start | bytes 245768 | tf_op jit(solution)/shard_map/ppermute | solution.py:102
  5.0 18.8 %collective-permute-start.1 = (bf16[448,512]{1,0:T(8,128)(2,1)S(1)}, bf16[448,512]{1,0:T(8,128)(2,1)S(1)}, u32[]{:S(2)}, u32[]{:S(2)}) collective-permute-start(bf16[448,512]{1,0:T(8,128)(2,1)S(1)} %get-tuple-element.14), channel_id=1, source_target_pairs={{0,16},{16,0},{1,17},{17,1},{2,18},{18,2},{3,19},{19,3},{4,20},{20... | collective-permute-start | bytes 1376264 | tf_op jit(solution)/shard_map/ppermute | solution.py:507
  12.5 7.4 %collective-permute-start.3 = (bf16[704,128]{1,0:T(8,128)(2,1)S(1)}, bf16[704,128]{1,0:T(8,128)(2,1)S(1)}, u32[]{:S(2)}, u32[]{:S(2)}) collective-permute-start(bf16[704,128]{1,0:T(8,128)(2,1)S(1)} %fusion.1), channel_id=1, source_target_pairs={{4,0},{8,4},{12,8},{5,1},{9,5},{13,9},{6,2},{10,6},{14,10},{7,3},{... | collective-permute-start | bytes 540680 | tf_op jit(solution)/shard_map/ppermute | solution.py:102
  20.0 3.9 %collective-permute-start.4 = (bf16[160,128]{1,0:T(8,128)(2,1)S(1)}, bf16[160,128]{1,0:T(8,128)(2,1)S(1)}, u32[]{:S(2)}, u32[]{:S(2)}) collective-permute-start(bf16[160,128]{1,0:T(8,128)(2,1)S(1)} %pad_maximum_fusion), channel_id=1, source_target_pairs={{0,16},{1,17},{2,18},{3,19},{4,20},{5,21},{6,22},{7,23},{8,24},{9,... | collective-permute-start | bytes 122888 | tf_op jit(solution)/shard_map/ppermute | solution.py:102
  23.9 2.0 %copy-start = (s32[1,2,10,10]{3,1,2,0:T(2,128)S(1)}, s32[1,2,10,10]{3,1,2,0:T(2,128)}, u32[]{:S(2)}) copy-start(s32[1,2,10,10]{3,1,2,0:T(2,128)} %param.5) | copy-start | bytes 2404
  24.5 6.5 %copy-start.1 = (s32[1,10,10]{2,0,1:T(1,128)S(1)}, s32[1,10,10]{2,0,1:T(1,128)}, u32[]{:S(2)}) copy-start(s32[1,10,10]{2,0,1:T(1,128)} %param.6) | copy-start | bytes 1204
  24.5 6.5 %collective-permute-start.5 = (f32[8,128]{1,0:T(8,128)S(1)}, f32[8,128]{1,0:T(8,128)S(1)}, u32[]{:S(2)}, u32[]{:S(2)}) collective-permute-start(f32[8,128]{1,0:T(8,128)S(1)} %shard_map.47), channel_id=1, source_target_pairs={{16,0},{17,1},{18,2},{19,3},{20,4},{21,5},{22,6},{23,7},{24,8},{25... | collective-permute-start | bytes 12296 | tf_op jit(solution)/shard_map/ppermute | solution.py:102
where the time goes:
time: 31.9 us; the launch traced here: 31.7 us
  starting transfers between devices  12.1 us (38%)
  Pallas kernels  11.2 us (35%)
  waiting for transfers between devices  7.96 us (25%)
    ppermute x4, starting transfers between devices, passed_along(): lax.ppermute(value, axis, [(source, source + steps) for source in range(i...  8.02 us
    ppermute x4, waiting for transfers between devices, passed_along(): lax.ppermute(value, axis, [(source, source + steps) for source in range(i...  7.95 us
    pallas_call x2, Pallas kernels, correlated(): pl.pallas_call(functools.partial(pair_kernel, slot, first_row, count_rows...  5.06 us
    ppermute x1, starting transfers between devices, body(): late_upper = late_lower = lax.ppermute(outs[1], 'gz', [(0, 1), (1, 0)])  2.75 us
    pallas_call x1, Pallas kernels, body(): pl.pallas_call(functools.partial(prepare_kernel, upper_rows, merged), out...  2.3 us
    pallas_call x1, Pallas kernels, body(): spectra = own_inner(active, tile, constants)  1.87 us
    pallas_call x1, Pallas kernels, body(): spectra, energy = own_rest(active, tile, below, beside, constants, spectra)  1.3 us
    ppermute x1, starting transfers between devices, body(): early_upper = early_lower = lax.ppermute(outs[0], ('gz', 'gy'), up + down)  1.29 us
  transfers between devices with their start and end apart: 6, of which 3 were waited for; matrix products, arithmetic and copies ran while one was open for 1% of the time, Pallas kernels for 24%

commit v1 on v0

--- a/solution.py
+++ b/solution.py
@@ -115,6 +115,21 @@
 def only_low(value):
     low = lax.broadcasted_iota(jnp.int32, value.shape, 1) < STRIDE
     return jnp.where(low, value.astype(F32), 0.0).astype(BF16)
+
+
+def working(count):
+    position = lax.axis_index("gz")
+    return position < count - 1, position > 0
+
+
+def start_all(copies):
+    for copy in copies:
+        copy.start()
+
+
+def wait_all(copies):
+    for copy in copies:
+        copy.wait()
 
 
 def parts(rows, first=0):
@@ -154,91 +169,77 @@
 
 def energies(chunk, blocks, first_row, patch_rows, mask, sums):
     for row in range(patch_rows + 1):
-        for block in range(blocks):
+        for block in blocks:
             pixels = chunk(first_row + row, block).astype(F32)
             sums[row : row + 1, block * PATCH : (block + 1) * PATCH] = jnp.sum(pixels * pixels, axis=0, keepdims=True)
-    both = sums[0:patch_rows, :] + sums[1 : patch_rows + 1, :]
-    total = sum(jnp.dot(term, mask, preferred_element_type=F32) for term in two_terms(both))
+    lanes = slice(blocks[0] * PATCH, (blocks[-1] + 1) * PATCH)
+    both = sums[0:patch_rows, lanes] + sums[1 : patch_rows + 1, lanes]
+    total = sum(jnp.dot(term, mask[lanes], preferred_element_type=F32) for term in two_terms(both))
     return total * (1.0 / (PATCH * PATCH))
 
 
-def prepare_kernel(upper_rows, merged, active, tile, peaks, constants, *refs):
+def prepare_kernel(upper_rows, merged, count, tile, peaks, *refs):
     rows, columns = tile.shape
     patch_rows = rows // STRIDE
     height = (upper_rows + 1) * STRIDE
     first_lower = upper_rows * STRIDE
     lower = rows - first_lower
-    sends = 2 if merged else 4
-    outs, (whole, top, left, held), (numbers, packed, sems) = refs[:sends], refs[sends : sends + 4], refs[sends + 4 :]
-    wide = columns - PATCH
+    sends = 3 if merged else 5
+    outs, (top, left), (numbers, packed, sems) = refs[:sends], refs[sends : sends + 2], refs[sends + 2 :]
+    up, down = outs[:3], outs[:2] if merged else outs[3:]
     blocks = columns // PATCH
-
-    def upwards(early, late, sem):
-        return [
-            pltpu.make_async_copy(tile.at[:height, :PATCH], early, sems.at[sem]),
-            pltpu.make_async_copy(tile.at[:height, PATCH:], late, sems.at[sem + 1]),
-        ]
-
-    def downwards(early, late, sem):
-        copies = [
-            (tile.at[:STRIDE, block * PATCH : (block + 1) * PATCH], early.at[block * STRIDE : (block + 1) * STRIDE, :])
-            for block in range(blocks)
-        ]
-        copies.append((tile.at[first_lower:, :wide], late.at[:lower, :]))
-        for half in range(2):
-            start = first_lower + half * lower // 2
-            copies.append(
-                (
-                    tile.at[start : start + lower // 2, wide:],
-                    late.at[lower : lower + lower // 2, half * PATCH : (half + 1) * PATCH],
-                )
-            )
-        return [pltpu.make_async_copy(a, b, sems.at[sem + k]) for k, (a, b) in enumerate(copies)]
-
-    def add_peaks(late):
+    inside = blocks - 2
+    _, has_before = working(count)
+
+    def lanes(block):
+        return slice(block * PATCH, (block + 1) * PATCH)
+
+    upwards = [
+        (tile.at[:height, lanes(0)], up[0]),
+        (tile.at[:height, PATCH : PATCH * (blocks - 1)], up[1]),
+        (tile.at[:height, lanes(blocks - 1)], up[2]),
+    ]
+    early, late = down
+    tall = height - lower
+    downwards = [(tile.at[:STRIDE, lanes(b)], early.at[b * STRIDE : (b + 1) * STRIDE, :]) for b in range(blocks)]
+    downwards.append((tile.at[first_lower:, : inside * PATCH], late.at[:lower, :]))
+    for k in range(2):
+        source = lanes(inside + k)
+        downwards.append((tile.at[first_lower : first_lower + tall, source], late.at[lower:, lanes(k)]))
+        at = lower + k * (lower - tall)
+        downwards.append((tile.at[first_lower + tall :, source], late.at[at : at + lower - tall, lanes(2)]))
+    peaks_at = lower + 2 * (lower - tall)
+
+    def add_peaks():
         packed[...] = jnp.zeros_like(packed)
         for i in range(patch_rows - upper_rows):
             packed[2 * i : 2 * i + 2, : peaks.shape[2]] = numbers[upper_rows + i].astype(F32)
-        late[lower + lower // 2 : lower + lower // 2 + SLOT, :PATCH] = packed[...].astype(BF16)
-
-    fixed = [
-        pltpu.make_async_copy(peaks, numbers, sems.at[0]),
-        pltpu.make_async_copy(tile, whole, sems.at[1]),
-        pltpu.make_async_copy(tile.at[:STRIDE, :], top, sems.at[2]),
-        pltpu.make_async_copy(tile.at[:, :PATCH], left, sems.at[3]),
-        pltpu.make_async_copy(constants, held, sems.at[4]),
-    ]
-    ups = upwards(outs[0], outs[1], 5)
-    downs = downwards(outs[-2], outs[-1], 7)
-
-    def start(copies):
-        for copy in copies:
-            copy.start()
-
-    def wait(copies):
-        for copy in copies:
-            copy.wait()
-
+        late[peaks_at : peaks_at + SLOT, lanes(2)] = packed[...].astype(BF16)
+
+    fixed = [(peaks, numbers), (tile.at[:STRIDE, :], top), (tile.at[:, :PATCH], left)]
+    groups = []
+    used = 0
+    for group in (upwards, downwards, fixed):
+        groups.append([pltpu.make_async_copy(a, b, sems.at[used + k]) for k, (a, b) in enumerate(group)])
+        used += len(group)
+    upwards, downwards, fixed = groups
     if merged:
-        pl.when(active[1] > 0)(lambda: start(ups))
-        pl.when(active[1] == 0)(lambda: start(downs))
+        pl.when(has_before)(lambda: start_all(upwards))
+        pl.when(jnp.logical_not(has_before))(lambda: start_all(downwards))
+        start_all(fixed)
+        fixed[0].wait()
+        pl.when(jnp.logical_not(has_before))(add_peaks)
+        pl.when(has_before)(lambda: wait_all(upwards))
+        pl.when(jnp.logical_not(has_before))(lambda: wait_all(downwards))
+        wait_all(fixed[1:])
     else:
-        start(ups)
-        start(downs)
-    start(fixed)
-    fixed[0].wait()
-    if merged:
-        pl.when(active[1] == 0)(lambda: add_peaks(outs[-1]))
-        pl.when(active[1] > 0)(lambda: wait(ups))
-        pl.when(active[1] == 0)(lambda: wait(downs))
-    else:
-        add_peaks(outs[-1])
-        wait(ups)
-        wait(downs)
-    wait(fixed[1:])
-
-
-def own_inner_kernel(upper_rows, active, tile, constants, spectra, once):
+        start_all(fixed + upwards + downwards)
+        fixed[0].wait()
+        add_peaks()
+        wait_all(fixed[1:] + upwards + downwards)
+
+
+def own_inner_kernel(upper_rows, count, source, tables_source, spectra, tile, constants, once, sems):
     rows, columns = tile.shape
     patch_rows = rows // STRIDE
     blocks = columns // PATCH
@@ -247,10 +248,17 @@
     def chunk(row, block):
         return tile[row * STRIDE : (row + 1) * STRIDE, block * PATCH : (block + 1) * PATCH]
 
+    copies = [
+        pltpu.make_async_copy(source, tile, sems.at[0]),
+        pltpu.make_async_copy(tables_source, constants, sems.at[1]),
+    ]
+    start_all(copies)
+    wait_all(copies)
+    active = working(count)
     inner = 2 * (blocks - 1) * PATCH
     for slot, (lowest, highest) in enumerate(((0, upper_rows), (upper_rows, patch_rows - 2))):
 
-        @pl.when(active[slot] > 0)
+        @pl.when(active[slot])
         def _(lowest=lowest, highest=highest):
             for step in range(lowest // 2, highest // 2):
                 columns_of = once.at[step % 2]
@@ -262,13 +270,14 @@
 
 
 def own_rest_kernel(
-    upper_rows, active, tile, below, beside, constants, started, spectra, energy, strip, sums, once
+    upper_rows, count, tile, below, beside, constants, started, spectra, energy, strip, sums, once
 ):
     rows, columns = tile.shape
     patch_rows = rows // STRIDE
     blocks = columns // PATCH
     table = Tables(constants, blocks)
     strip[...] = only_low(beside[...])
+    active = working(count)
 
     def chunk(row, block):
         at = slice(row * STRIDE, (row + 1) * STRIDE)
@@ -280,7 +289,7 @@
     inner = 2 * (blocks - 1) * PATCH
     for slot, (lowest, highest) in enumerate(((0, upper_rows), (upper_rows, patch_rows))):
 
-        @pl.when(active[slot] > 0)
+        @pl.when(active[slot])
         def _(slot=slot, lowest=lowest, highest=highest):
             for step in range(lowest // 2, highest // 2):
                 columns_of = once.at[step % 2]
@@ -298,7 +307,7 @@
                         before = spectra[step, middle : part.stop, :].astype(F32)
                         spectra[step, middle : part.stop, :] = (before + value[-size:]).astype(BF16)
             energy[slot, : highest - lowest, :] = energies(
-                chunk, blocks + 1, lowest, highest - lowest, table.mask(), sums
+                chunk, range(blocks + 1), lowest, highest - lowest, table.mask(), sums
             )
 
 
@@ -312,59 +321,80 @@
 
 
 def pair_kernel(
-    slot, first_row, patch_rows, patch_columns, active, peaks, early, late, beside, spectra, energy,
-    constants, out, strip, sums, once, crosses, inverse, peak, moments, offsets,
-    *surfaces
+    slot, chosen, first_row, patch_rows, patch_columns, count, peaks_source, early, late, last, beside, spectra, energy,
+    constants, out, peaks, sem, strip, sums, once, crosses, inverse, peak, moments, offsets, *surfaces
 ):
     flipped = slot == 1
     size = patch_rows * SLOT
     pairs = patch_columns // 2
     blocks = pairs
     table = Tables(constants, pairs)
-
-    @pl.when(active[slot] == 0)
+    active = working(count)[slot]
+    patches = range(2 * chosen[0], 2 * chosen[-1] + 2)
+
+    @pl.when(jnp.logical_not(active))
     def _():
         out[...] = jnp.zeros_like(out)
 
-    @pl.when(active[slot] > 0)
+    @pl.when(active)
     def _():
-        if flipped:
-            half = strip.shape[0] // 2
-            packed = beside[...].astype(F32)
-            low = lax.broadcasted_iota(jnp.int32, packed.shape, 1) < STRIDE
-            strip[:half, :] = jnp.where(low, packed, 0.0).astype(BF16)
-            strip[half:, :] = jnp.where(low, pltpu.roll(packed, STRIDE, 1), 0.0).astype(BF16)
-        else:
-            packed = beside[: strip.shape[0], :].astype(F32)
-            strip[...] = only_low(pltpu.roll(packed, STRIDE, 1))
+        fetch = pltpu.make_async_copy(peaks_source.at[:patch_rows], peaks, sem)
+        fetch.start()
+        if chosen[-1] == pairs - 1:
+            if flipped:
+                half = strip.shape[0] // 2
+                packed = beside[...].astype(F32)
+                low = lax.broadcasted_iota(jnp.int32, packed.shape, 1) < STRIDE
+                strip[:half, :] = jnp.where(low, packed, 0.0).astype(BF16)
+                strip[half:, :] = jnp.where(low, pltpu.roll(packed, STRIDE, 1), 0.0).astype(BF16)
+            else:
+                packed = beside[: strip.shape[0], :].astype(F32)
+                strip[...] = only_low(pltpu.roll(packed, STRIDE, 1))
+
+        def lanes_of(block):
+            return slice(block * PATCH, (block + 1) * PATCH)
 
         def chunk(row, block):
             at = slice(row * STRIDE, (row + 1) * STRIDE)
             if block == blocks:
                 return strip[at, :]
             if not flipped:
-                return early[at, :] if block == 0 else late[at, (block - 1) * PATCH : block * PATCH]
+                if block == 0:
+                    return early[at, :]
+                return last[at, :] if block == blocks - 1 else late[at, lanes_of(block - 1)]
             if row == patch_rows:
                 return early[block * STRIDE : (block + 1) * STRIDE, :]
-            if block < blocks - 1:
-                return late[at, block * PATCH : (block + 1) * PATCH]
-            side, place = divmod(row, patch_rows // 2)
-            top = (patch_rows + place) * STRIDE
-            return late[top : top + STRIDE, side * PATCH : (side + 1) * PATCH]
+            inside = blocks - 2
+            if block < inside:
+                return late[at, lanes_of(block)]
+            lower = patch_rows * STRIDE
+            tall = late.shape[0] - lower
+            start = row * STRIDE
+            if start < tall:
+                return late[lower + start : lower + start + STRIDE, lanes_of(block - inside)]
+            start += lower + (block - inside) * (lower - tall) - tall
+            return late[start : start + STRIDE, lanes_of(2)]
 
         row_of = lax.broadcasted_iota(jnp.int32, (SLOT, 2 * PATCH), 0)
         for step in range(patch_rows // 2):
             columns_of, cross, back = once.at[step % 2], crosses.at[step % 2], inverse.at[step % 2]
-            forward(chunk, 2 * step, table, columns_of)
-            for part in parts(columns_of.shape[0]):
+            forward(chunk, 2 * step, table, columns_of, chosen)
+            depth = columns_of.shape[0]
+            if len(chosen) == pairs:
+                rows = parts(depth)
+            else:
+                rows = parts(patches.stop * PATCH, patches.start * PATCH) + [slice(depth - 2 * SLOT, depth)]
+            for part in rows:
                 spectrum = jnp.dot(columns_of[part, :], table.second(), preferred_element_type=F32)
                 cross[part, :] = crossed(spectra[step + first_row // 2, part, :], spectrum, flipped)
-            for part in parts(columns_of.shape[0]):
+            for part in rows:
                 back[part, :] = jnp.dot(cross[part, :], table.third(), preferred_element_type=F32).astype(BF16)
             top = 2 * pairs * PATCH
             mid = back[top : top + 2 * SLOT, :PATCH].astype(F32)
             mid = jnp.concatenate([mid[:SLOT], mid[SLOT:]], 1)
-            for column in range(patch_columns):
+            if step == 0:
+                fetch.wait()
+            for column in patches:
                 a = (column // 2) * 2 * PATCH + (column % 2) * HALF
                 b = a + PATCH
                 right = jnp.concatenate(
@@ -381,7 +411,7 @@
                     lanes = slice(which * PATCH, (which + 1) * PATCH)
                     i = 2 * step + which
                     at = i * SLOT + column
-                    surface = surfaces[2 * column + which]
+                    surface = surfaces[2 * (column - patches.start) + which]
                     surface[EDGE : EDGE + PATCH, :] = value[:, lanes]
                     surface[:EDGE, :] = value[PATCH - EDGE :, lanes]
                     surface[EDGE + PATCH :, :] = value[:EDGE, lanes]
@@ -389,7 +419,7 @@
                     along = peaks[i, 1, column] + (EDGE - WIN // 2)
                     moments[at * 8 : at * 8 + 8, :] = surface[pl.ds(along, 8), :]
                     offsets[at : at + 1, :] = jnp.full((1, PATCH), peaks[i, 0, column], jnp.int32)
-        other = energies(chunk, blocks + 1, 0, patch_rows, table.mask(), sums)
+        other = energies(chunk, range(chosen[0], chosen[-1] + 2), 0, patch_rows, table.mask(), sums)
         scales = float(PATCH) ** 3 * jnp.sqrt((energy[slot, :patch_rows, :] + 1e-05) * (other + 1e-05))
 
         lane = lax.broadcasted_iota(jnp.int32, (1, PATCH), 1)
@@ -397,7 +427,7 @@
         for i in range(patch_rows):
             row = scales[i : i + 1, :]
             row = pltpu.roll(row, i * SLOT, 1) if i else row
-            scale = jnp.where((lane >= i * SLOT) & (lane < i * SLOT + patch_columns), row, scale)
+            scale = jnp.where((lane >= i * SLOT + patches.start) & (lane < i * SLOT + patches.stop), row, scale)
         peak_rows = peak[...]
         height = jnp.max(jnp.transpose(peak_rows), axis=0, keepdims=True) / scale + 1e-05
 
@@ -443,11 +473,12 @@
             out[:, size:] = jnp.zeros((8, PATCH - size), F32)
 
 
-def join_kernel(upper_rows, upper, lower, valid, out):
+def join_kernel(upper_rows, split, upper_left, upper_right, lower, valid, out):
     count, patch_rows, _, patch_columns = out.shape
+    lane = lax.broadcasted_iota(jnp.int32, upper_left.shape, 1) & (SLOT - 1)
+    upper = jnp.where(lane < split, upper_left[...], upper_right[...])
     for i in range(patch_rows):
-        source, at = (upper, i) if i < upper_rows else (lower, i - upper_rows)
-        value = source[...]
+        value, at = (upper, i) if i < upper_rows else (lower[...], i - upper_rows)
         turned = pltpu.roll(value, PATCH - at * SLOT, 1) if at else value
         keep = valid[i].astype(F32)
         for e in range(count):
@@ -465,15 +496,12 @@
     upper_height = first_lower + STRIDE
     lower_height = lower_rows * STRIDE + STRIDE
     count, height = lax.axis_size("gz"), lax.axis_size("gy")
-    position = lax.axis_index("gz")
-    active = jnp.stack([position < count - 1, position > 0]).astype(jnp.int32)
     peaks = jnp.transpose(peaks, (0, 2, 1, 3))[0]
     valid = jnp.transpose(valid, (1, 0, 2))
 
     constants = jnp.asarray(all_tables(columns // PATCH + 1, patch_columns), BF16)
 
     vmem = pl.BlockSpec(memory_space=pltpu.VMEM)
-    smem = pl.BlockSpec(memory_space=pltpu.SMEM)
 
     def grant(mib):
         return pltpu.CompilerParams(vmem_limit_bytes=mib << 20)
@@ -482,23 +510,28 @@
         return jax.ShapeDtypeStruct(dims, dtype)
 
     merged = count == 2
-    early, late = shape(upper_height, PATCH), shape(upper_height, columns - PATCH)
-    anywhere = pl.BlockSpec(memory_space=pltpu.HBM)
+    early, late, last = shape(upper_height, PATCH), shape(upper_height, columns - 2 * PATCH), shape(upper_height, PATCH)
+    hbm = pl.BlockSpec(memory_space=pltpu.HBM)
+
+    def held(value):
+        return pltpu.with_memory_space_constraint(value, pltpu.HBM)
+
+    copies = 3 + columns // PATCH + 5 + 3
     outs = pl.pallas_call(
-        functools.partial(prepare_kernel, upper_rows, merged),
-        out_shape=((early, late) if merged else (early, late) * 2)
-        + (shape(rows, columns), shape(STRIDE, columns), shape(rows, PATCH), shape(*constants.shape)),
-        in_specs=[smem] + [anywhere] * 3,
-        out_specs=(vmem,) * (6 if merged else 8),
+        functools.partial(prepare_kernel, upper_rows, merged, count),
+        out_shape=((early, late, last) if merged else (early, late, last, early, late))
+        + (shape(STRIDE, columns), shape(rows, PATCH)),
+        in_specs=[hbm] * 2,
+        out_specs=(vmem,) * (5 if merged else 7),
         scratch_shapes=[
             pltpu.VMEM(peaks.shape, jnp.int32),
             pltpu.VMEM((SLOT, PATCH), F32),
-            pltpu.SemaphoreType.DMA((7 + columns // PATCH + 3,)),
+            pltpu.SemaphoreType.DMA((copies,)),
         ],
         compiler_params=grant(1),
         name="prepare",
-    )(active, *(pltpu.with_memory_space_constraint(x, pltpu.HBM) for x in (tile, peaks, constants)))
-    tile, top, left, constants = outs[-4:]
+    )(held(tile), held(peaks))
+    top, left = outs[-2:]
 
     up = [((s + 1) * height + y, s * height + y) for s in range(count - 1) for y in range(height)]
     down = [(s * height + y + 1, (s + 1) * height + y) for s in range(count - 1) for y in range(height - 1)]
@@ -507,9 +540,10 @@
         late_upper = late_lower = lax.ppermute(outs[1], "gz", [(0, 1), (1, 0)])
     else:
         early_upper = lax.ppermute(outs[0], ("gz", "gy"), up)
-        early_lower = lax.ppermute(outs[2], ("gz", "gy"), down)
+        early_lower = lax.ppermute(outs[3], ("gz", "gy"), down)
         late_upper = passed_along(outs[1], "gz", -1)
-        late_lower = passed_along(outs[3], "gz", 1)
+        late_lower = passed_along(outs[4], "gz", 1)
+    last_upper = passed_along(outs[2], "gz", -1)
     below = passed_along(top, "gy", -1)
     others = jnp.pad(early_upper[:, :STRIDE], ((0, rows + STRIDE - upper_height), (0, 0)))
     ours = jnp.concatenate([left[:, :STRIDE], below[:, :STRIDE]], 0)
@@ -521,41 +555,43 @@
     width = columns + PATCH
     own_cost = pl.CostEstimate(flops=2_000_000_000, bytes_accessed=6_000_000, transcendentals=0)
     own_inner = pl.pallas_call(
-        functools.partial(own_inner_kernel, upper_rows),
-        out_shape=shape(steps, depth, 2 * PATCH),
-        in_specs=[smem] + [vmem] * 2,
-        out_specs=vmem,
-        scratch_shapes=[pltpu.VMEM((2, depth, 2 * PATCH), BF16)],
+        functools.partial(own_inner_kernel, upper_rows, count),
+        out_shape=(shape(steps, depth, 2 * PATCH), shape(rows, columns), shape(*constants.shape)),
+        in_specs=[hbm] * 2,
+        out_specs=(vmem,) * 3,
+        scratch_shapes=[pltpu.VMEM((2, depth, 2 * PATCH), BF16), pltpu.SemaphoreType.DMA((2,))],
         compiler_params=grant(6),
         cost_estimate=own_cost,
         name="own_inner",
     )
-    spectra = own_inner(active, tile, constants)
+    spectra, tile, constants = own_inner(held(tile), held(constants))
     own_rest = pl.pallas_call(
-        functools.partial(own_rest_kernel, upper_rows),
+        functools.partial(own_rest_kernel, upper_rows, count),
         out_shape=(shape(steps, depth, 2 * PATCH), shape(2, 8, PATCH, dtype=F32)),
-        in_specs=[smem] + [vmem] * 5,
+        in_specs=[vmem] * 5,
         out_specs=(vmem, vmem),
         scratch_shapes=[
             pltpu.VMEM((rows + STRIDE, PATCH), BF16),
             pltpu.VMEM((8, width), F32),
             pltpu.VMEM((2, depth, 2 * PATCH), BF16),
         ],
-        input_output_aliases={5: 0},
+        input_output_aliases={4: 0},
         compiler_params=grant(6),
         cost_estimate=own_cost,
         name="own_rest",
     )
-    spectra, energy = own_rest(active, tile, below, beside, constants, spectra)
-
-    def correlated(slot, first_row, count_rows, strip_rows, peaks_here, early, late, beside):
+    spectra, energy = own_rest(tile, below, beside, constants, spectra)
+
+    def correlated(slot, chosen, first_row, count_rows, strip_rows, peaks_here, *pieces):
         size = count_rows * SLOT
         return pl.pallas_call(
-            functools.partial(pair_kernel, slot, first_row, count_rows, patch_columns),
+            functools.partial(pair_kernel, slot, chosen, first_row, count_rows, patch_columns, count),
             out_shape=shape(8, PATCH, dtype=F32),
-            in_specs=[smem, smem] + [vmem] * 6,
+            in_specs=[pl.BlockSpec(memory_space=pl.ANY)] + [vmem] * 7,
             out_specs=vmem,
             scratch_shapes=[
+                pltpu.SMEM((count_rows, 2, patch_columns), jnp.int32),
+                pltpu.SemaphoreType.DMA,
                 pltpu.VMEM((strip_rows, PATCH), BF16),
                 pltpu.VMEM((8, width), F32),
                 pltpu.VMEM((2, depth, 2 * PATCH), BF16),
@@ -565,25 +601,32 @@
                 pltpu.VMEM((size * 8, PATCH), F32),
                 pltpu.VMEM((size, PATCH), jnp.int32),
             ]
-            + [pltpu.VMEM((PATCH + 2 * EDGE, PATCH), F32)] * (2 * patch_columns),
+            + [pltpu.VMEM((PATCH + 2 * EDGE, PATCH), F32)] * (4 * len(chosen)),
             compiler_params=grant(12),
             cost_estimate=pl.CostEstimate(flops=4_000_000_000, bytes_accessed=6_000_000, transcendentals=0),
-        )(active, peaks_here, early, late, beside, spectra, energy, constants)
-
-    at = lower_rows * STRIDE + lower_rows * STRIDE // 2
-    peaks_lower = late_lower[at : at + 2 * lower_rows, :patch_columns].astype(jnp.int32)
+        )(peaks_here, *pieces, spectra, energy, constants)
+
+    at = lower_rows * STRIDE + 2 * (2 * lower_rows * STRIDE - upper_height)
+    lanes = 2 * PATCH
+    peaks_lower = late_lower[at : at + 2 * lower_rows, lanes : lanes + patch_columns].astype(jnp.int32)
     peaks_lower = peaks_lower.reshape(lower_rows, 2, patch_columns)
-    lower = correlated(1, upper_rows, lower_rows, lower_height, peaks_lower, early_lower, late_lower, edge_lower)
+    lower = correlated(
+        1, range(pairs), upper_rows, lower_rows, lower_height, peaks_lower, early_lower, late_lower,
+        early_lower, edge_lower,
+    )
     lower = passed_along(lower, "gz", -1)
-    upper = correlated(0, 0, upper_rows, upper_height, peaks, early_upper, late_upper, beside)
+    split = pairs - 2
+    pieces = (early_upper, late_upper)
+    upper_left = correlated(0, range(split), 0, upper_rows, upper_height, peaks, *pieces, early_upper, early_upper)
+    upper_right = correlated(0, range(split, pairs), 0, upper_rows, upper_height, peaks, *pieces, last_upper, beside)
     fit = pl.pallas_call(
-        functools.partial(join_kernel, upper_rows),
+        functools.partial(join_kernel, upper_rows, 2 * split),
         out_shape=shape(6, patch_rows, 1, patch_columns, dtype=F32),
-        in_specs=[vmem] * 3,
+        in_specs=[vmem] * 4,
         out_specs=vmem,
         compiler_params=grant(1),
         name="join",
-    )(upper, lower, valid)
+    )(upper_left, upper_right, lower, valid)
     return jnp.transpose(fit, (2, 0, 1, 3))
 
 

time: 31.9 us -> 30.4 us (0.953)
  waiting for transfers between devices: 7.96 us -> 5.42 us
  starting transfers between devices: 12.1 us -> 13 us
    ppermute x4 -> x5, waiting for transfers between devices: 7.95 us -> 5.42 us  [passed_along(): lax.ppermute(value, axis, [(source, source + steps) for source in range(i...]
    ppermute x4 -> x5, starting transfers between devices: 8.02 us -> 9.06 us  [passed_along(): lax.ppermute(value, axis, [(source, source + steps) for source in range(i...]
    pallas_call x6 -> x7, Pallas kernels: 11.2 us -> 11.2 us  [the longest x3 5.73 us: correlated(): pl.pallas_call(functools.partial(pair_kernel, slot, chosen, first_row, co...]
  transfers between devices with their start and end apart: 6 -> 7, of which waited for: 3 -> 3; matrix products, arithmetic and copies ran while one was open for 1% -> 1% of each run, Pallas kernels for 24% -> 30%
where the time goes in v1:
time: 30.4 us; the launch traced here: 30.1 us
  starting transfers between devices  13 us (43%)
  Pallas kernels  11.2 us (37%)
  waiting for transfers between devices  5.42 us (18%)
    ppermute x5, starting transfers between devices, passed_along(): lax.ppermute(value, axis, [(source, source + steps) for source in range(i...  9.06 us
    pallas_call x3, Pallas kernels, correlated(): pl.pallas_call(functools.partial(pair_kernel, slot, chosen, first_row, co...  5.73 us
    ppermute x5, waiting for transfers between devices, passed_along(): lax.ppermute(value, axis, [(source, source + steps) for source in range(i...  5.42 us
    ppermute x1, starting transfers between devices, body(): late_upper = late_lower = lax.ppermute(outs[1], 'gz', [(0, 1), (1, 0)])  2.7 us
    pallas_call x1, Pallas kernels, body(): spectra, tile, constants = own_inner(held(tile), held(constants))  2.69 us
    pallas_call x1, Pallas kernels, body(): pl.pallas_call(functools.partial(prepare_kernel, upper_rows, merged, coun...  1.35 us
    ppermute x1, starting transfers between devices, body(): early_upper = early_lower = lax.ppermute(outs[0], ('gz', 'gy'), up + down)  1.29 us
    pallas_call x1, Pallas kernels, body(): spectra, energy = own_rest(tile, below, beside, constants, spectra)  0.76 us
  transfers between devices with their start and end apart: 7, of which 3 were waited for; matrix products, arithmetic and copies ran while one was open for 1% of the time, Pallas kernels for 30%

profile of v1, /device:TPU:1, one launch (start us, length us, event | category | flops | bytes accessed | tf_op | source)
XLA Modules:
  0.0 30.1 jit_solution(9145853821380682427)
XLA Ops:
  0.0 1.3 %prepare.1 = (bf16[448,128]{1,0:T(8,128)(2,1)S(1)}, bf16[448,384]{1,0:T(8,128)(2,1)S(1)}, bf16[448,128]{1,0:T(8,128)(2,1)S(1)}, bf16[64,640]{1,0:T(8,128)(2,1)S(1)}, bf16[640,128]{1,0:T(8,128)(2,1)S(1)}) custom-call(bf16[640,640]{1,0:T(8,128)(2,1)} %bitcast.16, s32[10,2,10]{2,1,0:T(2,128)} %bitcast.12), custom_call_target="tpu_custom_call" | custom-call | tf_op jit(solution)/shard_map/prepare/pallas_call | solution.py:520
  1.4 1.3 %collective-permute-start = (bf16[448,128]{1,0:T(8,128)(2,1)S(1)}, bf16[448,128]{1,0:T(8,128)(2,1)S(1)}, u32[]{:S(2)}, u32[]{:S(2)}) collective-permute-start(bf16[448,128]{1,0:T(8,128)(2,1)S(1)} %get-tuple-element.15), channel_id=1, source_target_pairs={{16,0},{17,1},{18,2},{19,3},{1,16},{2,17},{3,18},{20,4},{21,5},{22... | collective-permute-start | bytes 344072 | tf_op jit(solution)/shard_map/ppermute | solution.py:539
  2.7 1.3 %collective-permute-start.2 = (bf16[64,640]{1,0:T(8,128)(2,1)S(1)}, bf16[64,640]{1,0:T(8,128)(2,1)S(1)}, u32[]{:S(2)}, u32[]{:S(2)}) collective-permute-start(bf16[64,640]{1,0:T(8,128)(2,1)S(1)} %get-tuple-element.18), channel_id=1, source_target_pairs={{1,0},{2,1},{3,2},{5,4},{6,5},{7,6},{9,8},{10,9},{11,10},{13,12},{... | collective-permute-start | bytes 245768 | tf_op jit(solution)/shard_map/ppermute | solution.py:102
  4.0 2.7 %collective-permute-start.1 = (bf16[448,384]{1,0:T(8,128)(2,1)S(1)}, bf16[448,384]{1,0:T(8,128)(2,1)S(1)}, u32[]{:S(2)}, u32[]{:S(2)}) collective-permute-start(bf16[448,384]{1,0:T(8,128)(2,1)S(1)} %get-tuple-element.16), channel_id=1, source_target_pairs={{0,16},{16,0},{1,17},{17,1},{2,18},{18,2},{3,19},{19,3},{4,20},{20... | collective-permute-start | bytes 1032200 | tf_op jit(solution)/shard_map/ppermute | solution.py:540
  6.7 1.3 %collective-permute-start.4 = (bf16[448,128]{1,0:T(8,128)(2,1)S(1)}, bf16[448,128]{1,0:T(8,128)(2,1)S(1)}, u32[]{:S(2)}, u32[]{:S(2)}) collective-permute-start(bf16[448,128]{1,0:T(8,128)(2,1)S(1)} %get-tuple-element.24), channel_id=1, source_target_pairs={{16,0},{17,1},{18,2},{19,3},{20,4},{21,5},{22,6},{23,7},{24,8},{25... | collective-permute-start | bytes 344072 | tf_op jit(solution)/shard_map/ppermute | solution.py:102
  7.9 3.3 %collective-permute-done.2.below = bf16[64,640]{1,0:T(8,128)(2,1)S(1)} collective-permute-done((bf16[64,640]{1,0:T(8,128)(2,1)S(1)}, bf16[64,640]{1,0:T(8,128)(2,1)S(1)}, u32[]{:S(2)}, u32[]{:S(2)}) %collective-permute-start.2) | collective-permute-done | bytes 81952 | tf_op jit(solution)/shard_map/ppermute | solution.py:102
  11.3 0.0 collective-permute-done.early.last.beside
  11.3 0.1 fusion.1
  11.4 2.9 %collective-permute-start.3 = (bf16[704,128]{1,0:T(8,128)(2,1)S(1)}, bf16[704,128]{1,0:T(8,128)(2,1)S(1)}, u32[]{:S(2)}, u32[]{:S(2)}) collective-permute-start(bf16[704,128]{1,0:T(8,128)(2,1)S(1)} %fusion.1), channel_id=1, source_target_pairs={{4,0},{8,4},{12,8},{5,1},{9,5},{13,9},{6,2},{10,6},{14,10},{7,3},{... | collective-permute-start | bytes 540680 | tf_op jit(solution)/shard_map/ppermute | solution.py:102
  14.3 2.7 %own_inner.1 = (bf16[5,1312,256]{2,1,0:T(8,128)(2,1)S(1)}, bf16[640,640]{1,0:T(8,128)(2,1)S(1)}, bf16[1360,256]{1,0:T(8,128)(2,1)S(1)}) custom-call(bf16[640,640]{1,0:T(8,128)(2,1)} %bitcast.17, bf16[1360,256]{1,0:T(8,128)(2,1)} %constant.5.clone.tables_source), custom_call_target="tpu_custom_call" | custom-call | flops 2000000000 | bytes 6000000 | tf_op jit(solution)/shard_map/own_inner/pallas_call | solution.py:567
  17.0 1.8 %collective-permute-done.3.beside = bf16[704,128]{1,0:T(8,128)(2,1)S(1)} collective-permute-done((bf16[704,128]{1,0:T(8,128)(2,1)S(1)}, bf16[704,128]{1,0:T(8,128)(2,1)S(1)}, u32[]{:S(2)}, u32[]{:S(2)}) %collective-permute-start.3) | collective-permute-done | bytes 180256 | tf_op jit(solution)/shard_map/ppermute | solution.py:102
  18.8 0.1 pad_maximum_fusion
  18.9 2.3 %collective-permute-start.5 = (bf16[160,128]{1,0:T(8,128)(2,1)S(1)}, bf16[160,128]{1,0:T(8,128)(2,1)S(1)}, u32[]{:S(2)}, u32[]{:S(2)}) collective-permute-start(bf16[160,128]{1,0:T(8,128)(2,1)S(1)} %pad_maximum_fusion), channel_id=1, source_target_pairs={{0,16},{1,17},{2,18},{3,19},{4,20},{5,21},{6,22},{7,23},{8,24},{9,... | collective-permute-start | bytes 122888 | tf_op jit(solution)/shard_map/ppermute | solution.py:102
  21.2 0.8 %own_rest.1 = (bf16[5,1312,256]{2,1,0:T(8,128)(2,1)S(1)}, f32[2,8,128]{2,1,0:T(8,128)S(1)}) custom-call(bf16[640,640]{1,0:T(8,128)(2,1)S(1)} %get-tuple-element.17.tile, bf16[64,640]{1,0:T(8,128)(2,1)S(1)} %collective-permute-done.2.below, bf16[704,128]{1,0:T(8,128)(2,1)S(1)} %collective-permute-done.3.beside, ...), custom_call_target="tpu_custom_call", output_to_operand_aliasing={{0}: (4, {})} | custom-call | flops 2000000000 | bytes 6000000 | tf_op jit(solution)/shard_map/own_rest/pallas_call | solution.py:583
  21.9 0.0 collective-permute-done.1.late
  22.0 0.3 collective-permute-done.5.beside
  22.3 0.0 copy-start
  22.3 1.3 %collective-permute-start.6 = (f32[8,128]{1,0:T(8,128)S(1)}, f32[8,128]{1,0:T(8,128)S(1)}, u32[]{:S(2)}, u32[]{:S(2)}) collective-permute-start(f32[8,128]{1,0:T(8,128)S(1)} %shard_map.48), channel_id=1, source_target_pairs={{16,0},{17,1},{18,2},{19,3},{20,4},{21,5},{22,6},{23,7},{24,8},{25... | collective-permute-start | bytes 12296 | tf_op jit(solution)/shard_map/ppermute | solution.py:102
  23.6 0.0 copy-done
  23.6 3.1 %shard_map.46.upper_left = f32[8,128]{1,0:T(8,128)S(1)} custom-call(s32[10,2,10]{2,1,0:T(2,128)S(1)} %bitcast.13, bf16[448,128]{1,0:T(8,128)(2,1)S(1)} %collective-permute-done.early.last.beside, bf16[448,384]{1,0:T(8,128)(2,1)S(1)} %collective-permute-done.1.late, bf16[448,128]{1,0:T(8,128)(2,1)S(1)} %collective-permute-done.early.last.beside, ...), custom_call_target="tpu_custom_call" | custom-call | flops 4000000000 | bytes 6000000 | tf_op jit(solution)/shard_map/pallas_call | solution.py:587
  26.7 0.0 copy-start.1
  26.7 0.0 collective-permute-done.4.last
  26.7 2.6 %shard_map.47.upper_right = f32[8,128]{1,0:T(8,128)S(1)} custom-call(s32[10,2,10]{2,1,0:T(2,128)S(1)} %bitcast.14, bf16[448,128]{1,0:T(8,128)(2,1)S(1)} %collective-permute-done.early.last.beside, bf16[448,384]{1,0:T(8,128)(2,1)S(1)} %collective-permute-done.1.late, bf16[448,128]{1,0:T(8,128)(2,1)S(1)} %collective-permute-done.4.last, ...), custom_call_target="tpu_custom_call" | custom-call | flops 4000000000 | bytes 6000000 | tf_op jit(solution)/shard_map/pallas_call | solution.py:587
  29.4 0.0 collective-permute-done.6.lower
  29.4 0.0 copy-done.1
  29.4 0.7 %join.1 = f32[6,10,1,10]{3,2,1,0:T(1,128)} custom-call(f32[8,128]{1,0:T(8,128)S(1)} %shard_map.46.upper_left, f32[8,128]{1,0:T(8,128)S(1)} %shard_map.47.upper_right, f32[8,128]{1,0:T(8,128)S(1)} %collective-permute-done.6.lower, s32[10,1,10]{2,1,0:T(1,128)S(1)} %bitcast.15), custom_call_target="tpu_custom_call" | custom-call | tf_op jit(solution)/shard_map/join/pallas_call | solution.py:622
  (5 shorter events, 0.0 us)
Async XLA Ops:
  1.4 9.9 %collective-permute-start = (bf16[448,128]{1,0:T(8,128)(2,1)S(1)}, bf16[448,128]{1,0:T(8,128)(2,1)S(1)}, u32[]{:S(2)}, u32[]{:S(2)}) collective-permute-start(bf16[448,128]{1,0:T(8,128)(2,1)S(1)} %get-tuple-element.15), channel_id=1, source_target_pairs={{16,0},{17,1},{18,2},{19,3},{1,16},{2,17},{3,18},{20,4},{21,5},{22... | collective-permute-start | bytes 344072 | tf_op jit(solution)/shard_map/ppermute | solution.py:539
  2.7 8.6 %collective-permute-start.2 = (bf16[64,640]{1,0:T(8,128)(2,1)S(1)}, bf16[64,640]{1,0:T(8,128)(2,1)S(1)}, u32[]{:S(2)}, u32[]{:S(2)}) collective-permute-start(bf16[64,640]{1,0:T(8,128)(2,1)S(1)} %get-tuple-element.18), channel_id=1, source_target_pairs={{1,0},{2,1},{3,2},{5,4},{6,5},{7,6},{9,8},{10,9},{11,10},{13,12},{... | collective-permute-start | bytes 245768 | tf_op jit(solution)/shard_map/ppermute | solution.py:102
  4.0 18.0 %collective-permute-start.1 = (bf16[448,384]{1,0:T(8,128)(2,1)S(1)}, bf16[448,384]{1,0:T(8,128)(2,1)S(1)}, u32[]{:S(2)}, u32[]{:S(2)}) collective-permute-start(bf16[448,384]{1,0:T(8,128)(2,1)S(1)} %get-tuple-element.16), channel_id=1, source_target_pairs={{0,16},{16,0},{1,17},{17,1},{2,18},{18,2},{3,19},{19,3},{4,20},{20... | collective-permute-start | bytes 1032200 | tf_op jit(solution)/shard_map/ppermute | solution.py:540
  6.7 20.1 %collective-permute-start.4 = (bf16[448,128]{1,0:T(8,128)(2,1)S(1)}, bf16[448,128]{1,0:T(8,128)(2,1)S(1)}, u32[]{:S(2)}, u32[]{:S(2)}) collective-permute-start(bf16[448,128]{1,0:T(8,128)(2,1)S(1)} %get-tuple-element.24), channel_id=1, source_target_pairs={{16,0},{17,1},{18,2},{19,3},{20,4},{21,5},{22,6},{23,7},{24,8},{25... | collective-permute-start | bytes 344072 | tf_op jit(solution)/shard_map/ppermute | solution.py:102
  11.4 7.4 %collective-permute-start.3 = (bf16[704,128]{1,0:T(8,128)(2,1)S(1)}, bf16[704,128]{1,0:T(8,128)(2,1)S(1)}, u32[]{:S(2)}, u32[]{:S(2)}) collective-permute-start(bf16[704,128]{1,0:T(8,128)(2,1)S(1)} %fusion.1), channel_id=1, source_target_pairs={{4,0},{8,4},{12,8},{5,1},{9,5},{13,9},{6,2},{10,6},{14,10},{7,3},{... | collective-permute-start | bytes 540680 | tf_op jit(solution)/shard_map/ppermute | solution.py:102
  18.9 3.4 %collective-permute-start.5 = (bf16[160,128]{1,0:T(8,128)(2,1)S(1)}, bf16[160,128]{1,0:T(8,128)(2,1)S(1)}, u32[]{:S(2)}, u32[]{:S(2)}) collective-permute-start(bf16[160,128]{1,0:T(8,128)(2,1)S(1)} %pad_maximum_fusion), channel_id=1, source_target_pairs={{0,16},{1,17},{2,18},{3,19},{4,20},{5,21},{6,22},{7,23},{8,24},{9,... | collective-permute-start | bytes 122888 | tf_op jit(solution)/shard_map/ppermute | solution.py:102
  22.3 1.3 %copy-start = (s32[1,2,10,10]{3,1,2,0:T(2,128)S(1)}, s32[1,2,10,10]{3,1,2,0:T(2,128)}, u32[]{:S(2)}) copy-start(s32[1,2,10,10]{3,1,2,0:T(2,128)} %param.5) | copy-start | bytes 2404
  22.3 7.1 %collective-permute-start.6 = (f32[8,128]{1,0:T(8,128)S(1)}, f32[8,128]{1,0:T(8,128)S(1)}, u32[]{:S(2)}, u32[]{:S(2)}) collective-permute-start(f32[8,128]{1,0:T(8,128)S(1)} %shard_map.48), channel_id=1, source_target_pairs={{16,0},{17,1},{18,2},{19,3},{20,4},{21,5},{22,6},{23,7},{24,8},{25... | collective-permute-start | bytes 12296 | tf_op jit(solution)/shard_map/ppermute | solution.py:102
  26.7 2.7 %copy-start.1 = (s32[1,10,10]{2,0,1:T(1,128)S(1)}, s32[1,10,10]{2,0,1:T(1,128)}, u32[]{:S(2)}) copy-start(s32[1,10,10]{2,0,1:T(1,128)} %param.6) | copy-start | bytes 1204

commit v2 on v1

--- a/solution.py
+++ b/solution.py
@@ -100,11 +100,6 @@
     count = lax.axis_size(axis)
     initial, last = (max(0, -steps), min(count, count - steps))
     return lax.ppermute(value, axis, [(source, source + steps) for source in range(initial, last)])
-
-
-def side_by_side(value):
-    rows = value.shape[0] // 2
-    return jnp.concatenate([value[:rows, :STRIDE], value[rows:, :STRIDE]], 1)
 
 
 def two_terms(value):
@@ -185,7 +180,7 @@
     first_lower = upper_rows * STRIDE
     lower = rows - first_lower
     sends = 3 if merged else 5
-    outs, (top, left), (numbers, packed, sems) = refs[:sends], refs[sends : sends + 2], refs[sends + 2 :]
+    outs, (side, top, left), (numbers, packed, sems) = refs[:sends], refs[sends : sends + 3], refs[sends + 3 :]
     up, down = outs[:3], outs[:2] if merged else outs[3:]
     blocks = columns // PATCH
     inside = blocks - 2
@@ -216,7 +211,12 @@
             packed[2 * i : 2 * i + 2, : peaks.shape[2]] = numbers[upper_rows + i].astype(F32)
         late[peaks_at : peaks_at + SLOT, lanes(2)] = packed[...].astype(BF16)
 
-    fixed = [(peaks, numbers), (tile.at[:STRIDE, :], top), (tile.at[:, :PATCH], left)]
+    fixed = [
+        (peaks, numbers),
+        (tile.at[first_lower:, :PATCH], side),
+        (tile.at[:STRIDE, :], top),
+        (tile.at[:, :PATCH], left),
+    ]
     groups = []
     used = 0
     for group in (upwards, downwards, fixed):
@@ -239,7 +239,9 @@
         wait_all(fixed[1:] + upwards + downwards)
 
 
-def own_inner_kernel(upper_rows, count, source, tables_source, spectra, tile, constants, once, sems):
+def own_inner_kernel(
+    upper_rows, left_pairs, count, source, tables_source, spectra, tile, constants, energy, sums, once, sems
+):
     rows, columns = tile.shape
     patch_rows = rows // STRIDE
     blocks = columns // PATCH
@@ -259,7 +261,7 @@
     for slot, (lowest, highest) in enumerate(((0, upper_rows), (upper_rows, patch_rows - 2))):
 
         @pl.when(active[slot])
-        def _(lowest=lowest, highest=highest):
+        def _(slot=slot, lowest=lowest, highest=highest):
             for step in range(lowest // 2, highest // 2):
                 columns_of = once.at[step % 2]
                 forward(chunk, 2 * step, table, columns_of, range(blocks - 1))
@@ -267,10 +269,43 @@
                 for part in parts(inner) + [slice(depth - 2 * SLOT, depth)]:
                     value = jnp.dot(columns_of[part, :], table.second(), preferred_element_type=F32)
                     spectra[step, part, :] = value.astype(BF16)
+            if slot == 0:
+                energy[0, :upper_rows, :] = energies(
+                    chunk, range(left_pairs + 1), 0, upper_rows, table.mask(), sums
+                )
+
+
+def own_below_kernel(
+    upper_rows, left_pairs, count, tile, below, constants, started, early_energy, spectra, energy, sums, once
+):
+    rows, columns = tile.shape
+    patch_rows = rows // STRIDE
+    blocks = columns // PATCH
+    table = Tables(constants, blocks)
+
+    def chunk(row, block):
+        lanes = slice(block * PATCH, (block + 1) * PATCH)
+        return tile[row * STRIDE : (row + 1) * STRIDE, lanes] if row < patch_rows else below[:, lanes]
+
+    inner = 2 * (blocks - 1) * PATCH
+    step = patch_rows // 2 - 1
+
+    @pl.when(working(count)[1])
+    def _():
+        columns_of = once
+        forward(chunk, 2 * step, table, columns_of, range(blocks - 1))
+        depth = columns_of.shape[0]
+        for part in parts(inner) + [slice(depth - 2 * SLOT, depth)]:
+            value = jnp.dot(columns_of[part, :], table.second(), preferred_element_type=F32)
+            spectra[step, part, :] = value.astype(BF16)
+        energy[1, : patch_rows - upper_rows, :] = energies(
+            chunk, range(left_pairs + 1), upper_rows, patch_rows - upper_rows, table.mask(), sums
+        )
 
 
 def own_rest_kernel(
-    upper_rows, count, tile, below, beside, constants, started, spectra, energy, strip, sums, once
+    upper_rows, left_pairs, count, tile, below, beside, constants, started, after_upper, after_lower, spectra, energy,
+    strip, sums, once
 ):
     rows, columns = tile.shape
     patch_rows = rows // STRIDE
@@ -294,12 +329,11 @@
             for step in range(lowest // 2, highest // 2):
                 columns_of = once.at[step % 2]
                 depth = columns_of.shape[0]
-                last = step == patch_rows // 2 - 1
-                forward(chunk, 2 * step, table, columns_of, None if last else [blocks - 1])
-                for part in parts(depth, 0 if last else inner):
+                forward(chunk, 2 * step, table, columns_of, [blocks - 1])
+                for part in parts(depth, inner):
                     value = jnp.dot(columns_of[part, :], table.second(), preferred_element_type=F32)
                     middle = max(part.start, depth - 2 * SLOT)
-                    if last or part.stop <= middle:
+                    if part.stop <= middle:
                         spectra[step, part, :] = value.astype(BF16)
                     else:
                         size = part.stop - middle
@@ -307,7 +341,7 @@
                         before = spectra[step, middle : part.stop, :].astype(F32)
                         spectra[step, middle : part.stop, :] = (before + value[-size:]).astype(BF16)
             energy[slot, : highest - lowest, :] = energies(
-                chunk, range(blocks + 1), lowest, highest - lowest, table.mask(), sums
+                chunk, range(left_pairs, blocks + 1), lowest, highest - lowest, table.mask(), sums
             )
 
 
@@ -321,8 +355,8 @@
 
 
 def pair_kernel(
-    slot, chosen, first_row, patch_rows, patch_columns, count, peaks_source, early, late, last, beside, spectra, energy,
-    constants, out, peaks, sem, strip, sums, once, crosses, inverse, peak, moments, offsets, *surfaces
+    slot, chosen, first_row, patch_rows, patch_columns, count, corner, peaks_source, early, late, last, beside, left, spectra,
+    energy, constants, out, peaks, sem, strip, sums, once, crosses, inverse, peak, moments, offsets, *surfaces
 ):
     flipped = slot == 1
     size = patch_rows * SLOT
@@ -342,11 +376,10 @@
         fetch.start()
         if chosen[-1] == pairs - 1:
             if flipped:
-                half = strip.shape[0] // 2
-                packed = beside[...].astype(F32)
-                low = lax.broadcasted_iota(jnp.int32, packed.shape, 1) < STRIDE
-                strip[:half, :] = jnp.where(low, packed, 0.0).astype(BF16)
-                strip[half:, :] = jnp.where(low, pltpu.roll(packed, STRIDE, 1), 0.0).astype(BF16)
+                most = patch_rows * STRIDE
+                strip[:most, :] = only_low(last[...])
+                packed = beside[corner : corner + STRIDE, :].astype(F32)
+                strip[most:, :] = only_low(pltpu.roll(packed, STRIDE, 1))
             else:
                 packed = beside[: strip.shape[0], :].astype(F32)
                 strip[...] = only_low(pltpu.roll(packed, STRIDE, 1))
@@ -468,17 +501,20 @@
         factor = jnp.zeros((8, size), F32)
         for e, norm in enumerate(norms):
             factor = jnp.where(e_row == e, 1.0 / norm, factor)
-        out[:, :size] = total * factor / (scale * height)[:, :size]
+        result = total * factor / (scale * height)[:, :size]
+        if chosen[0] > 0:
+            slot_lane = lax.broadcasted_iota(jnp.int32, (8, size), 1) & (SLOT - 1)
+            result = jnp.where(slot_lane < patches.start, left[:, :size], result)
+        out[:, :size] = result
         if size < PATCH:
             out[:, size:] = jnp.zeros((8, PATCH - size), F32)
 
 
-def join_kernel(upper_rows, split, upper_left, upper_right, lower, valid, out):
+def join_kernel(upper_rows, upper, lower, valid, out):
     count, patch_rows, _, patch_columns = out.shape
-    lane = lax.broadcasted_iota(jnp.int32, upper_left.shape, 1) & (SLOT - 1)
-    upper = jnp.where(lane < split, upper_left[...], upper_right[...])
     for i in range(patch_rows):
-        value, at = (upper, i) if i < upper_rows else (lower[...], i - upper_rows)
+        source, at = (upper, i) if i < upper_rows else (lower, i - upper_rows)
+        value = source[...]
         turned = pltpu.roll(value, PATCH - at * SLOT, 1) if at else value
         keep = valid[i].astype(F32)
         for e in range(count):
@@ -516,13 +552,13 @@
     def held(value):
         return pltpu.with_memory_space_constraint(value, pltpu.HBM)
 
-    copies = 3 + columns // PATCH + 5 + 3
+    copies = 3 + columns // PATCH + 5 + 4
     outs = pl.pallas_call(
         functools.partial(prepare_kernel, upper_rows, merged, count),
         out_shape=((early, late, last) if merged else (early, late, last, early, late))
-        + (shape(STRIDE, columns), shape(rows, PATCH)),
+        + (shape(rows - first_lower, PATCH), shape(STRIDE, columns), shape(rows, PATCH)),
         in_specs=[hbm] * 2,
-        out_specs=(vmem,) * (5 if merged else 7),
+        out_specs=(vmem,) * (6 if merged else 8),
         scratch_shapes=[
             pltpu.VMEM(peaks.shape, jnp.int32),
             pltpu.VMEM((SLOT, PATCH), F32),
@@ -531,10 +567,13 @@
         compiler_params=grant(1),
         name="prepare",
     )(held(tile), held(peaks))
-    top, left = outs[-2:]
+    side, top, left = outs[-3:]
 
     up = [((s + 1) * height + y, s * height + y) for s in range(count - 1) for y in range(height)]
     down = [(s * height + y + 1, (s + 1) * height + y) for s in range(count - 1) for y in range(height - 1)]
+    across = lax.axis_size("gx")
+    slant = [(s * across + x + 1, (s + 1) * across + x) for s in range(count - 1) for x in range(across - 1)]
+    side = lax.ppermute(side, ("gz", "gx"), slant)
     if merged:
         early_upper = early_lower = lax.ppermute(outs[0], ("gz", "gy"), up + down)
         late_upper = late_lower = lax.ppermute(outs[1], "gz", [(0, 1), (1, 0)])
@@ -544,50 +583,37 @@
         late_upper = passed_along(outs[1], "gz", -1)
         late_lower = passed_along(outs[4], "gz", 1)
     last_upper = passed_along(outs[2], "gz", -1)
-    below = passed_along(top, "gy", -1)
-    others = jnp.pad(early_upper[:, :STRIDE], ((0, rows + STRIDE - upper_height), (0, 0)))
+    steps_up = [(s * height + y + 1, s * height + y) for s in range(1, count) for y in range(height - 1)]
+    below = lax.ppermute(top, ("gz", "gy"), steps_up)
+    others = jnp.concatenate([early_upper[:, :STRIDE], early_lower[:STRIDE, :STRIDE]], 0)
+    others = jnp.pad(others, ((0, rows - upper_height), (0, 0)))
     ours = jnp.concatenate([left[:, :STRIDE], below[:, :STRIDE]], 0)
     beside = passed_along(jnp.concatenate([ours, others], 1), "gx", -1)
-    edge_lower = passed_along(side_by_side(beside[first_lower : rows + STRIDE]), "gz", 1)
-
     steps = patch_rows // 2
     depth = 2 * pairs * PATCH + 2 * SLOT
     width = columns + PATCH
+    split = pairs - 2
     own_cost = pl.CostEstimate(flops=2_000_000_000, bytes_accessed=6_000_000, transcendentals=0)
     own_inner = pl.pallas_call(
-        functools.partial(own_inner_kernel, upper_rows, count),
-        out_shape=(shape(steps, depth, 2 * PATCH), shape(rows, columns), shape(*constants.shape)),
+        functools.partial(own_inner_kernel, upper_rows, split, count),
+        out_shape=(
+            shape(steps, depth, 2 * PATCH), shape(rows, columns), shape(*constants.shape), shape(2, 8, PATCH, dtype=F32)
+        ),
         in_specs=[hbm] * 2,
-        out_specs=(vmem,) * 3,
-        scratch_shapes=[pltpu.VMEM((2, depth, 2 * PATCH), BF16), pltpu.SemaphoreType.DMA((2,))],
+        out_specs=(vmem,) * 4,
+        scratch_shapes=[pltpu.VMEM((8, width), F32), pltpu.VMEM((2, depth, 2 * PATCH), BF16), pltpu.SemaphoreType.DMA((2,))],
         compiler_params=grant(6),
         cost_estimate=own_cost,
         name="own_inner",
     )
-    spectra, tile, constants = own_inner(held(tile), held(constants))
-    own_rest = pl.pallas_call(
-        functools.partial(own_rest_kernel, upper_rows, count),
-        out_shape=(shape(steps, depth, 2 * PATCH), shape(2, 8, PATCH, dtype=F32)),
-        in_specs=[vmem] * 5,
-        out_specs=(vmem, vmem),
-        scratch_shapes=[
-            pltpu.VMEM((rows + STRIDE, PATCH), BF16),
-            pltpu.VMEM((8, width), F32),
-            pltpu.VMEM((2, depth, 2 * PATCH), BF16),
-        ],
-        input_output_aliases={4: 0},
-        compiler_params=grant(6),
-        cost_estimate=own_cost,
-        name="own_rest",
-    )
-    spectra, energy = own_rest(tile, below, beside, constants, spectra)
-
-    def correlated(slot, chosen, first_row, count_rows, strip_rows, peaks_here, *pieces):
+    spectra, tile, constants, energy_left = own_inner(held(tile), held(constants))
+
+    def correlated(slot, chosen, first_row, count_rows, strip_rows, peaks_here, spectra, energy, *pieces):
         size = count_rows * SLOT
         return pl.pallas_call(
-            functools.partial(pair_kernel, slot, chosen, first_row, count_rows, patch_columns, count),
+            functools.partial(pair_kernel, slot, chosen, first_row, count_rows, patch_columns, count, upper_height),
             out_shape=shape(8, PATCH, dtype=F32),
-            in_specs=[pl.BlockSpec(memory_space=pl.ANY)] + [vmem] * 7,
+            in_specs=[pl.BlockSpec(memory_space=pl.ANY)] + [vmem] * 8,
             out_specs=vmem,
             scratch_shapes=[
                 pltpu.SMEM((count_rows, 2, patch_columns), jnp.int32),
@@ -606,27 +632,60 @@
             cost_estimate=pl.CostEstimate(flops=4_000_000_000, bytes_accessed=6_000_000, transcendentals=0),
         )(peaks_here, *pieces, spectra, energy, constants)
 
+    own_below = pl.pallas_call(
+        functools.partial(own_below_kernel, upper_rows, split, count),
+        out_shape=(shape(steps, depth, 2 * PATCH), shape(2, 8, PATCH, dtype=F32)),
+        in_specs=[vmem] * 5,
+        out_specs=(vmem, vmem),
+        scratch_shapes=[pltpu.VMEM((8, width), F32), pltpu.VMEM((depth, 2 * PATCH), BF16)],
+        input_output_aliases={3: 0, 4: 1},
+        compiler_params=grant(4),
+        cost_estimate=own_cost,
+        name="own_below",
+    )
+    spectra, energy_left = own_below(tile, below, constants, spectra, energy_left)
     at = lower_rows * STRIDE + 2 * (2 * lower_rows * STRIDE - upper_height)
     lanes = 2 * PATCH
     peaks_lower = late_lower[at : at + 2 * lower_rows, lanes : lanes + patch_columns].astype(jnp.int32)
     peaks_lower = peaks_lower.reshape(lower_rows, 2, patch_columns)
-    lower = correlated(
-        1, range(pairs), upper_rows, lower_rows, lower_height, peaks_lower, early_lower, late_lower,
-        early_lower, edge_lower,
+    upper_part = (0, upper_rows, upper_height, peaks)
+    lower_part = (upper_rows, lower_rows, lower_height, peaks_lower)
+    nothing = energy_left[0]
+    upper_left = correlated(
+        0, range(split), *upper_part, spectra, energy_left, early_upper, late_upper, nothing, nothing, nothing
     )
+    lower_left = correlated(
+        1, range(split), *lower_part, spectra, energy_left, early_lower, late_lower, nothing, nothing, nothing
+    )
+    own_rest = pl.pallas_call(
+        functools.partial(own_rest_kernel, upper_rows, split, count),
+        out_shape=(shape(steps, depth, 2 * PATCH), shape(2, 8, PATCH, dtype=F32)),
+        in_specs=[vmem] * 7,
+        out_specs=(vmem, vmem),
+        scratch_shapes=[
+            pltpu.VMEM((rows + STRIDE, PATCH), BF16),
+            pltpu.VMEM((8, width), F32),
+            pltpu.VMEM((2, depth, 2 * PATCH), BF16),
+        ],
+        input_output_aliases={4: 0},
+        compiler_params=grant(6),
+        cost_estimate=own_cost,
+        name="own_rest",
+    )
+    spectra, energy = own_rest(tile, below, beside, constants, spectra, upper_left, lower_left)
+
+    rest = range(split, pairs)
+    lower = correlated(1, rest, *lower_part, spectra, energy, early_lower, late_lower, side, beside, lower_left)
     lower = passed_along(lower, "gz", -1)
-    split = pairs - 2
-    pieces = (early_upper, late_upper)
-    upper_left = correlated(0, range(split), 0, upper_rows, upper_height, peaks, *pieces, early_upper, early_upper)
-    upper_right = correlated(0, range(split, pairs), 0, upper_rows, upper_height, peaks, *pieces, last_upper, beside)
+    upper = correlated(0, rest, *upper_part, spectra, energy, early_upper, late_upper, last_upper, beside, upper_left)
     fit = pl.pallas_call(
-        functools.partial(join_kernel, upper_rows, 2 * split),
+        functools.partial(join_kernel, upper_rows),
         out_shape=shape(6, patch_rows, 1, patch_columns, dtype=F32),
-        in_specs=[vmem] * 4,
+        in_specs=[vmem] * 3,
         out_specs=vmem,
         compiler_params=grant(1),
         name="join",
-    )(upper_left, upper_right, lower, valid)
+    )(upper, lower, valid)
     return jnp.transpose(fit, (2, 0, 1, 3))
 
 

time: 30.4 us -> 32.7 us (1.076)
  the two profiles are of different devices: /device:TPU:1 before, /device:TPU:28 now
where the time goes in v2:
time: 32.7 us; the launch traced here: 32.4 us
  starting transfers between devices  14.1 us (43%)
  Pallas kernels  11.3 us (35%)
  waiting for transfers between devices  6.63 us (20%)
    pallas_call x4, Pallas kernels, correlated(): pl.pallas_call(functools.partial(pair_kernel, slot, chosen, first_row, co...  5.76 us
    ppermute x1, waiting for transfers between devices, body(): late_upper = late_lower = lax.ppermute(outs[1], 'gz', [(0, 1), (1, 0)])  5.07 us
    ppermute x3, starting transfers between devices, passed_along(): lax.ppermute(value, axis, [(source, source + steps) for source in range(i...  4.5 us
    ppermute x1, starting transfers between devices, body(): early_upper = early_lower = lax.ppermute(outs[0], ('gz', 'gy'), up + down)  3.49 us
    pallas_call x1, Pallas kernels, body(): own_inner(held(tile), held(constants))  2.74 us
    ppermute x1, starting transfers between devices, body(): side = lax.ppermute(side, ('gz', 'gx'), slant)  2.74 us
    ppermute x1, starting transfers between devices, body(): late_upper = late_lower = lax.ppermute(outs[1], 'gz', [(0, 1), (1, 0)])  2.71 us
    ppermute x3, waiting for transfers between devices, passed_along(): lax.ppermute(value, axis, [(source, source + steps) for source in range(i...  1.55 us
  transfers between devices with their start and end apart: 7, of which 2 were waited for; matrix products, arithmetic and copies ran while one was open for 1% of the time, Pallas kernels for 28%

profile of v2, /device:TPU:28, one launch (start us, length us, event | category | flops | bytes accessed | tf_op | source)
XLA Modules:
  0.0 32.4 jit_solution(8698497144769275334)
XLA Ops:
  0.0 1.4 %prepare.1 = (bf16[448,128]{1,0:T(8,128)(2,1)S(1)}, bf16[448,384]{1,0:T(8,128)(2,1)S(1)}, bf16[448,128]{1,0:T(8,128)(2,1)S(1)}, bf16[256,128]{1,0:T(8,128)(2,1)S...) custom-call(bf16[640,640]{1,0:T(8,128)(2,1)} %bitcast.18, s32[10,2,10]{2,1,0:T(2,128)} %bitcast.14), custom_call_target="tpu_custom_call" | custom-call | tf_op jit(solution)/shard_map/prepare/pallas_call | solution.py:556
  1.4 2.7 %collective-permute-start.5 = (bf16[256,128]{1,0:T(8,128)(2,1)S(1)}, bf16[256,128]{1,0:T(8,128)(2,1)S(1)}, u32[]{:S(2)}, u32[]{:S(2)}) collective-permute-start(bf16[256,128]{1,0:T(8,128)(2,1)S(1)} %get-tuple-element.32), channel_id=1, source_target_pairs={{4,16},{8,20},{12,24},{5,17},{9,21},{13,25},{6,18},{10,22},{14,26}... | collective-permute-start | bytes 196616 | tf_op jit(solution)/shard_map/ppermute | solution.py:576
  4.2 0.7 %collective-permute-start.3 = (bf16[64,640]{1,0:T(8,128)(2,1)S(1)}, bf16[64,640]{1,0:T(8,128)(2,1)S(1)}, u32[]{:S(2)}, u32[]{:S(2)}) collective-permute-start(bf16[64,640]{1,0:T(8,128)(2,1)S(1)} %get-tuple-element.23), channel_id=1, source_target_pairs={{17,16},{18,17},{19,18},{21,20},{22,21},{23,22},{25,24},{26,25},{2... | collective-permute-start | bytes 245768 | tf_op jit(solution)/shard_map/ppermute | solution.py:587
  4.8 3.5 %collective-permute-start = (bf16[448,128]{1,0:T(8,128)(2,1)S(1)}, bf16[448,128]{1,0:T(8,128)(2,1)S(1)}, u32[]{:S(2)}, u32[]{:S(2)}) collective-permute-start(bf16[448,128]{1,0:T(8,128)(2,1)S(1)} %get-tuple-element.19), channel_id=1, source_target_pairs={{16,0},{17,1},{18,2},{19,3},{1,16},{2,17},{3,18},{20,4},{21,5},{22... | collective-permute-start | bytes 344072 | tf_op jit(solution)/shard_map/ppermute | solution.py:578
  8.3 1.3 %collective-permute-start.2 = (bf16[448,128]{1,0:T(8,128)(2,1)S(1)}, bf16[448,128]{1,0:T(8,128)(2,1)S(1)}, u32[]{:S(2)}, u32[]{:S(2)}) collective-permute-start(bf16[448,128]{1,0:T(8,128)(2,1)S(1)} %get-tuple-element.21), channel_id=1, source_target_pairs={{16,0},{17,1},{18,2},{19,3},{20,4},{21,5},{22,6},{23,7},{24,8},{25... | collective-permute-start | bytes 344072 | tf_op jit(solution)/shard_map/ppermute | solution.py:102
  9.6 2.7 %collective-permute-start.1 = (bf16[448,384]{1,0:T(8,128)(2,1)S(1)}, bf16[448,384]{1,0:T(8,128)(2,1)S(1)}, u32[]{:S(2)}, u32[]{:S(2)}) collective-permute-start(bf16[448,384]{1,0:T(8,128)(2,1)S(1)} %get-tuple-element.20), channel_id=1, source_target_pairs={{0,16},{16,0},{1,17},{17,1},{2,18},{18,2},{3,19},{19,3},{4,20},{20... | collective-permute-start | bytes 1032200 | tf_op jit(solution)/shard_map/ppermute | solution.py:579
  12.3 2.7 %own_inner.1 = (bf16[5,1312,256]{2,1,0:T(8,128)(2,1)S(1)}, bf16[640,640]{1,0:T(8,128)(2,1)S(1)}, bf16[1360,256]{1,0:T(8,128)(2,1)S(1)}, f32[2,8,128]{2,1,0:T(8,128)S(1)}) custom-call(bf16[640,640]{1,0:T(8,128)(2,1)} %bitcast.19, bf16[1360,256]{1,0:T(8,128)(2,1)} %constant.5.clone.tables_source), custom_call_target="tpu_custom_call" | custom-call | flops 2000000000 | bytes 6000000 | tf_op jit(solution)/shard_map/own_inner/pallas_call | solution.py:609
  15.1 0.0 collective-permute-done.3.below
  15.1 0.0 copy-start
  15.2 0.0 collective-permute-done.early
  15.2 0.1 pad_maximum_fusion
  15.3 1.9 %collective-permute-start.4 = (bf16[704,128]{1,0:T(8,128)(2,1)S(1)}, bf16[704,128]{1,0:T(8,128)(2,1)S(1)}, u32[]{:S(2)}, u32[]{:S(2)}) collective-permute-start(bf16[704,128]{1,0:T(8,128)(2,1)S(1)} %pad_maximum_fusion), channel_id=1, source_target_pairs={{4,0},{8,4},{12,8},{5,1},{9,5},{13,9},{6,2},{10,6},{14,10},{7,3},{... | collective-permute-start | bytes 540680 | tf_op jit(solution)/shard_map/ppermute | solution.py:102
  17.3 5.1 %collective-permute-done.1.late = bf16[448,384]{1,0:T(8,128)(2,1)S(1)} collective-permute-done((bf16[448,384]{1,0:T(8,128)(2,1)S(1)}, bf16[448,384]{1,0:T(8,128)(2,1)S(1)}, u32[]{:S(2)}, u32[]{:S(2)}) %collective-permute-start.1) | collective-permute-done | bytes 344096 | tf_op jit(solution)/shard_map/ppermute | solution.py:579
  22.3 0.0 copy-done
  22.4 3.1 %shard_map.46.after_upper.left = f32[8,128]{1,0:T(8,128)S(1)} custom-call(s32[10,2,10]{2,1,0:T(2,128)S(1)} %bitcast.15, bf16[448,128]{1,0:T(8,128)(2,1)S(1)} %collective-permute-done.early, bf16[448,384]{1,0:T(8,128)(2,1)S(1)} %collective-permute-done.1.late, f32[8,128]{1,0:T(8,128)S(1)} %slice_bitcast_fusion.last.beside.left, ...), custom_call_target="tpu_custom_call" | custom-call | flops 4000000000 | bytes 6000000 | tf_op jit(solution)/shard_map/pallas_call | solution.py:613
  25.5 0.0 collective-permute-done.4.beside
  25.5 0.7 %own_rest.1 = (bf16[5,1312,256]{2,1,0:T(8,128)(2,1)S(1)}, f32[2,8,128]{2,1,0:T(8,128)S(1)}) custom-call(bf16[640,640]{1,0:T(8,128)(2,1)S(1)} %get-tuple-element.24.tile, bf16[64,640]{1,0:T(8,128)(2,1)S(1)} %collective-permute-done.3.below, bf16[704,128]{1,0:T(8,128)(2,1)S(1)} %collective-permute-done.4.beside, ...), custom_call_target="tpu_custom_call", output_to_operand_aliasing={{0}: (4, {})} | custom-call | flops 2000000000 | bytes 6000000 | tf_op jit(solution)/shard_map/own_rest/pallas_call | solution.py:675
  26.2 0.0 collective-permute-done.5.last
  26.2 0.0 copy-start.1
  26.2 1.3 %collective-permute-start.6 = (f32[8,128]{1,0:T(8,128)S(1)}, f32[8,128]{1,0:T(8,128)S(1)}, u32[]{:S(2)}, u32[]{:S(2)}) collective-permute-start(f32[8,128]{1,0:T(8,128)S(1)} %shard_map.49), channel_id=1, source_target_pairs={{16,0},{17,1},{18,2},{19,3},{20,4},{21,5},{22,6},{23,7},{24,8},{25... | collective-permute-start | bytes 12296 | tf_op jit(solution)/shard_map/ppermute | solution.py:102
  27.5 0.0 collective-permute-done.2.last
  27.5 2.6 %shard_map.48.upper = f32[8,128]{1,0:T(8,128)S(1)} custom-call(s32[10,2,10]{2,1,0:T(2,128)S(1)} %bitcast.16, bf16[448,128]{1,0:T(8,128)(2,1)S(1)} %collective-permute-done.early, bf16[448,384]{1,0:T(8,128)(2,1)S(1)} %collective-permute-done.1.late, bf16[448,128]{1,0:T(8,128)(2,1)S(1)} %collective-permute-done.2.last, ...), custom_call_target="tpu_custom_call" | custom-call | flops 4000000000 | bytes 6000000 | tf_op jit(solution)/shard_map/pallas_call | solution.py:613
  30.2 1.5 %collective-permute-done.6.lower = f32[8,128]{1,0:T(8,128)S(1)} collective-permute-done((f32[8,128]{1,0:T(8,128)S(1)}, f32[8,128]{1,0:T(8,128)S(1)}, u32[]{:S(2)}, u32[]{:S(2)}) %collective-permute-start.6) | collective-permute-done | bytes 4128 | tf_op jit(solution)/shard_map/ppermute | solution.py:102
  31.7 0.0 copy-done.1
  31.7 0.7 %join.1 = f32[6,10,1,10]{3,2,1,0:T(1,128)} custom-call(f32[8,128]{1,0:T(8,128)S(1)} %shard_map.48.upper, f32[8,128]{1,0:T(8,128)S(1)} %collective-permute-done.6.lower, s32[10,1,10]{2,1,0:T(1,128)S(1)} %bitcast.17), custom_call_target="tpu_custom_call" | custom-call | tf_op jit(solution)/shard_map/join/pallas_call | solution.py:681
  (9 shorter events, 0.1 us)
Async XLA Ops:
  1.4 24.8 %collective-permute-start.5 = (bf16[256,128]{1,0:T(8,128)(2,1)S(1)}, bf16[256,128]{1,0:T(8,128)(2,1)S(1)}, u32[]{:S(2)}, u32[]{:S(2)}) collective-permute-start(bf16[256,128]{1,0:T(8,128)(2,1)S(1)} %get-tuple-element.32), channel_id=1, source_target_pairs={{4,16},{8,20},{12,24},{5,17},{9,21},{13,25},{6,18},{10,22},{14,26}... | collective-permute-start | bytes 196616 | tf_op jit(solution)/shard_map/ppermute | solution.py:576
  4.2 10.9 %collective-permute-start.3 = (bf16[64,640]{1,0:T(8,128)(2,1)S(1)}, bf16[64,640]{1,0:T(8,128)(2,1)S(1)}, u32[]{:S(2)}, u32[]{:S(2)}) collective-permute-start(bf16[64,640]{1,0:T(8,128)(2,1)S(1)} %get-tuple-element.23), channel_id=1, source_target_pairs={{17,16},{18,17},{19,18},{21,20},{22,21},{23,22},{25,24},{26,25},{2... | collective-permute-start | bytes 245768 | tf_op jit(solution)/shard_map/ppermute | solution.py:587
  4.8 10.3 %collective-permute-start = (bf16[448,128]{1,0:T(8,128)(2,1)S(1)}, bf16[448,128]{1,0:T(8,128)(2,1)S(1)}, u32[]{:S(2)}, u32[]{:S(2)}) collective-permute-start(bf16[448,128]{1,0:T(8,128)(2,1)S(1)} %get-tuple-element.19), channel_id=1, source_target_pairs={{16,0},{17,1},{18,2},{19,3},{1,16},{2,17},{3,18},{20,4},{21,5},{22... | collective-permute-start | bytes 344072 | tf_op jit(solution)/shard_map/ppermute | solution.py:578
  8.3 19.2 %collective-permute-start.2 = (bf16[448,128]{1,0:T(8,128)(2,1)S(1)}, bf16[448,128]{1,0:T(8,128)(2,1)S(1)}, u32[]{:S(2)}, u32[]{:S(2)}) collective-permute-start(bf16[448,128]{1,0:T(8,128)(2,1)S(1)} %get-tuple-element.21), channel_id=1, source_target_pairs={{16,0},{17,1},{18,2},{19,3},{20,4},{21,5},{22,6},{23,7},{24,8},{25... | collective-permute-start | bytes 344072 | tf_op jit(solution)/shard_map/ppermute | solution.py:102
  9.6 12.7 %collective-permute-start.1 = (bf16[448,384]{1,0:T(8,128)(2,1)S(1)}, bf16[448,384]{1,0:T(8,128)(2,1)S(1)}, u32[]{:S(2)}, u32[]{:S(2)}) collective-permute-start(bf16[448,384]{1,0:T(8,128)(2,1)S(1)} %get-tuple-element.20), channel_id=1, source_target_pairs={{0,16},{16,0},{1,17},{17,1},{2,18},{18,2},{3,19},{19,3},{4,20},{20... | collective-permute-start | bytes 1032200 | tf_op jit(solution)/shard_map/ppermute | solution.py:579
  15.1 7.3 %copy-start = (s32[1,2,10,10]{3,1,2,0:T(2,128)S(1)}, s32[1,2,10,10]{3,1,2,0:T(2,128)}, u32[]{:S(2)}) copy-start(s32[1,2,10,10]{3,1,2,0:T(2,128)} %param.5) | copy-start | bytes 2404
  15.3 10.1 %collective-permute-start.4 = (bf16[704,128]{1,0:T(8,128)(2,1)S(1)}, bf16[704,128]{1,0:T(8,128)(2,1)S(1)}, u32[]{:S(2)}, u32[]{:S(2)}) collective-permute-start(bf16[704,128]{1,0:T(8,128)(2,1)S(1)} %pad_maximum_fusion), channel_id=1, source_target_pairs={{4,0},{8,4},{12,8},{5,1},{9,5},{13,9},{6,2},{10,6},{14,10},{7,3},{... | collective-permute-start | bytes 540680 | tf_op jit(solution)/shard_map/ppermute | solution.py:102
  26.2 5.5 %copy-start.1 = (s32[1,10,10]{2,0,1:T(1,128)S(1)}, s32[1,10,10]{2,0,1:T(1,128)}, u32[]{:S(2)}) copy-start(s32[1,10,10]{2,0,1:T(1,128)} %param.6) | copy-start | bytes 1204
  26.2 5.5 %collective-permute-start.6 = (f32[8,128]{1,0:T(8,128)S(1)}, f32[8,128]{1,0:T(8,128)S(1)}, u32[]{:S(2)}, u32[]{:S(2)}) collective-permute-start(f32[8,128]{1,0:T(8,128)S(1)} %shard_map.49), channel_id=1, source_target_pairs={{16,0},{17,1},{18,2},{19,3},{20,4},{21,5},{22,6},{23,7},{24,8},{25... | collective-permute-start | bytes 12296 | tf_op jit(solution)/shard_map/ppermute | solution.py:102

commit v3 on v2

--- a/solution.py
+++ b/solution.py
@@ -276,7 +276,7 @@
 
 
 def own_below_kernel(
-    upper_rows, left_pairs, count, tile, below, constants, started, early_energy, spectra, energy, sums, once
+    count, tile, below, constants, started, spectra, once
 ):
     rows, columns = tile.shape
     patch_rows = rows // STRIDE
@@ -298,20 +298,18 @@
         for part in parts(inner) + [slice(depth - 2 * SLOT, depth)]:
             value = jnp.dot(columns_of[part, :], table.second(), preferred_element_type=F32)
             spectra[step, part, :] = value.astype(BF16)
-        energy[1, : patch_rows - upper_rows, :] = energies(
-            chunk, range(left_pairs + 1), upper_rows, patch_rows - upper_rows, table.mask(), sums
-        )
 
 
 def own_rest_kernel(
-    upper_rows, left_pairs, count, tile, below, beside, constants, started, after_upper, after_lower, spectra, energy,
+    upper_rows, left_pairs, count, tile, below, beside, corners, constants, started, after_upper, spectra, energy,
     strip, sums, once
 ):
     rows, columns = tile.shape
     patch_rows = rows // STRIDE
     blocks = columns // PATCH
     table = Tables(constants, blocks)
-    strip[...] = only_low(beside[...])
+    strip[:rows, :] = only_low(beside[...])
+    strip[rows:, :] = only_low(corners[...])
     active = working(count)
 
     def chunk(row, block):
@@ -341,7 +339,7 @@
                         before = spectra[step, middle : part.stop, :].astype(F32)
                         spectra[step, middle : part.stop, :] = (before + value[-size:]).astype(BF16)
             energy[slot, : highest - lowest, :] = energies(
-                chunk, range(left_pairs, blocks + 1), lowest, highest - lowest, table.mask(), sums
+                chunk, range(0 if slot else left_pairs, blocks + 1), lowest, highest - lowest, table.mask(), sums
             )
 
 
@@ -355,7 +353,7 @@
 
 
 def pair_kernel(
-    slot, chosen, first_row, patch_rows, patch_columns, count, corner, peaks_source, early, late, last, beside, left, spectra,
+    slot, chosen, first_row, patch_rows, patch_columns, count, peaks_source, early, late, last, beside, left, spectra,
     energy, constants, out, peaks, sem, strip, sums, once, crosses, inverse, peak, moments, offsets, *surfaces
 ):
     flipped = slot == 1
@@ -378,7 +376,7 @@
             if flipped:
                 most = patch_rows * STRIDE
                 strip[:most, :] = only_low(last[...])
-                packed = beside[corner : corner + STRIDE, :].astype(F32)
+                packed = beside[...].astype(F32)
                 strip[most:, :] = only_low(pltpu.roll(packed, STRIDE, 1))
             else:
                 packed = beside[: strip.shape[0], :].astype(F32)
@@ -585,10 +583,12 @@
     last_upper = passed_along(outs[2], "gz", -1)
     steps_up = [(s * height + y + 1, s * height + y) for s in range(1, count) for y in range(height - 1)]
     below = lax.ppermute(top, ("gz", "gy"), steps_up)
-    others = jnp.concatenate([early_upper[:, :STRIDE], early_lower[:STRIDE, :STRIDE]], 0)
-    others = jnp.pad(others, ((0, rows - upper_height), (0, 0)))
-    ours = jnp.concatenate([left[:, :STRIDE], below[:, :STRIDE]], 0)
-    beside = passed_along(jnp.concatenate([ours, others], 1), "gx", -1)
+    others = jnp.pad(early_upper[:, :STRIDE], ((0, rows - upper_height), (0, 0)))
+    beside = passed_along(jnp.concatenate([left[:, :STRIDE], others], 1), "gx", -1)
+    corners = jnp.concatenate([below[:, :STRIDE], early_lower[:STRIDE, :STRIDE]], 1)
+    level = [(s * across + x + 1, s * across + x) for s in range(1, count) for x in range(across - 1)]
+    corners = lax.ppermute(corners, ("gz", "gx"), level)
+
     steps = patch_rows // 2
     depth = 2 * pairs * PATCH + 2 * SLOT
     width = columns + PATCH
@@ -611,7 +611,7 @@
     def correlated(slot, chosen, first_row, count_rows, strip_rows, peaks_here, spectra, energy, *pieces):
         size = count_rows * SLOT
         return pl.pallas_call(
-            functools.partial(pair_kernel, slot, chosen, first_row, count_rows, patch_columns, count, upper_height),
+            functools.partial(pair_kernel, slot, chosen, first_row, count_rows, patch_columns, count),
             out_shape=shape(8, PATCH, dtype=F32),
             in_specs=[pl.BlockSpec(memory_space=pl.ANY)] + [vmem] * 8,
             out_specs=vmem,
@@ -633,17 +633,17 @@
         )(peaks_here, *pieces, spectra, energy, constants)
 
     own_below = pl.pallas_call(
-        functools.partial(own_below_kernel, upper_rows, split, count),
-        out_shape=(shape(steps, depth, 2 * PATCH), shape(2, 8, PATCH, dtype=F32)),
-        in_specs=[vmem] * 5,
-        out_specs=(vmem, vmem),
-        scratch_shapes=[pltpu.VMEM((8, width), F32), pltpu.VMEM((depth, 2 * PATCH), BF16)],
-        input_output_aliases={3: 0, 4: 1},
+        functools.partial(own_below_kernel, count),
+        out_shape=shape(steps, depth, 2 * PATCH),
+        in_specs=[vmem] * 4,
+        out_specs=vmem,
+        scratch_shapes=[pltpu.VMEM((depth, 2 * PATCH), BF16)],
+        input_output_aliases={3: 0},
         compiler_params=grant(4),
         cost_estimate=own_cost,
         name="own_below",
     )
-    spectra, energy_left = own_below(tile, below, constants, spectra, energy_left)
+    spectra = own_below(tile, below, constants, spectra)
     at = lower_rows * STRIDE + 2 * (2 * lower_rows * STRIDE - upper_height)
     lanes = 2 * PATCH
     peaks_lower = late_lower[at : at + 2 * lower_rows, lanes : lanes + patch_columns].astype(jnp.int32)
@@ -653,9 +653,6 @@
     nothing = energy_left[0]
     upper_left = correlated(
         0, range(split), *upper_part, spectra, energy_left, early_upper, late_upper, nothing, nothing, nothing
-    )
-    lower_left = correlated(
-        1, range(split), *lower_part, spectra, energy_left, early_lower, late_lower, nothing, nothing, nothing
     )
     own_rest = pl.pallas_call(
         functools.partial(own_rest_kernel, upper_rows, split, count),
@@ -667,15 +664,15 @@
             pltpu.VMEM((8, width), F32),
             pltpu.VMEM((2, depth, 2 * PATCH), BF16),
         ],
-        input_output_aliases={4: 0},
+        input_output_aliases={5: 0},
         compiler_params=grant(6),
         cost_estimate=own_cost,
         name="own_rest",
     )
-    spectra, energy = own_rest(tile, below, beside, constants, spectra, upper_left, lower_left)
+    spectra, energy = own_rest(tile, below, beside, corners, constants, spectra, upper_left)
 
     rest = range(split, pairs)
-    lower = correlated(1, rest, *lower_part, spectra, energy, early_lower, late_lower, side, beside, lower_left)
+    lower = correlated(1, range(pairs), *lower_part, spectra, energy, early_lower, late_lower, side, corners, nothing)
     lower = passed_along(lower, "gz", -1)
     upper = correlated(0, rest, *upper_part, spectra, energy, early_upper, late_upper, last_upper, beside, upper_left)
     fit = pl.pallas_call(

time: 32.7 us -> 32.9 us (level)
  the two profiles are of different devices: /device:TPU:28 before, /device:TPU:17 now
where the time goes in v3:
time: 32.9 us; the launch traced here: 32.6 us
  starting transfers between devices  15 us (46%)
  Pallas kernels  11.3 us (34%)
  waiting for transfers between devices  5.87 us (18%)
    ppermute x3, waiting for transfers between devices, passed_along(): lax.ppermute(value, axis, [(source, source + steps) for source in range(i...  5.86 us
    pallas_call x3, Pallas kernels, correlated(): pl.pallas_call(functools.partial(pair_kernel, slot, chosen, first_row, co...  5.77 us
    ppermute x1, starting transfers between devices, body(): side = lax.ppermute(side, ('gz', 'gx'), slant)  4.64 us
    ppermute x3, starting transfers between devices, passed_along(): lax.ppermute(value, axis, [(source, source + steps) for source in range(i...  4.5 us
    ppermute x1, starting transfers between devices, body(): early_upper = early_lower = lax.ppermute(outs[0], ('gz', 'gy'), up + down)  4.38 us
    pallas_call x1, Pallas kernels, body(): own_inner(held(tile), held(constants))  2.75 us
    pallas_call x1, Pallas kernels, body(): pl.pallas_call(functools.partial(prepare_kernel, upper_rows, merged, coun...  1.39 us
    pallas_call x1, Pallas kernels, body(): pl.pallas_call(functools.partial(join_kernel, upper_rows), out_shape=shap...  0.69 us
  transfers between devices with their start and end apart: 8, of which 2 were waited for; matrix products, arithmetic and copies ran while one was open for 1% of the time, Pallas kernels for 28%

profile of v3, /device:TPU:17, one launch (start us, length us, event | category | flops | bytes accessed | tf_op | source)
XLA Modules:
  0.0 32.6 jit_solution(1804950354968767236)
XLA Ops:
  0.0 1.4 %prepare.1 = (bf16[448,128]{1,0:T(8,128)(2,1)S(1)}, bf16[448,384]{1,0:T(8,128)(2,1)S(1)}, bf16[448,128]{1,0:T(8,128)(2,1)S(1)}, bf16[256,128]{1,0:T(8,128)(2,1)S...) custom-call(bf16[640,640]{1,0:T(8,128)(2,1)} %bitcast.18, s32[10,2,10]{2,1,0:T(2,128)} %bitcast.14), custom_call_target="tpu_custom_call" | custom-call | tf_op jit(solution)/shard_map/prepare/pallas_call | solution.py:554
  1.4 0.7 %collective-permute-start.4 = (bf16[64,640]{1,0:T(8,128)(2,1)S(1)}, bf16[64,640]{1,0:T(8,128)(2,1)S(1)}, u32[]{:S(2)}, u32[]{:S(2)}) collective-permute-start(bf16[64,640]{1,0:T(8,128)(2,1)S(1)} %get-tuple-element.23), channel_id=1, source_target_pairs={{17,16},{18,17},{19,18},{21,20},{22,21},{23,22},{25,24},{26,25},{2... | collective-permute-start | bytes 245768 | tf_op jit(solution)/shard_map/ppermute | solution.py:585
  2.1 4.4 %collective-permute-start = (bf16[448,128]{1,0:T(8,128)(2,1)S(1)}, bf16[448,128]{1,0:T(8,128)(2,1)S(1)}, u32[]{:S(2)}, u32[]{:S(2)}) collective-permute-start(bf16[448,128]{1,0:T(8,128)(2,1)S(1)} %get-tuple-element.17), channel_id=1, source_target_pairs={{16,0},{17,1},{18,2},{19,3},{1,16},{2,17},{3,18},{20,4},{21,5},{22... | collective-permute-start | bytes 344072 | tf_op jit(solution)/shard_map/ppermute | solution.py:576
  6.5 0.2 collective-permute-start.1
  6.7 4.6 %collective-permute-start.6 = (bf16[256,128]{1,0:T(8,128)(2,1)S(1)}, bf16[256,128]{1,0:T(8,128)(2,1)S(1)}, u32[]{:S(2)}, u32[]{:S(2)}) collective-permute-start(bf16[256,128]{1,0:T(8,128)(2,1)S(1)} %get-tuple-element.28), channel_id=1, source_target_pairs={{4,16},{8,20},{12,24},{5,17},{9,21},{13,25},{6,18},{10,22},{14,26}... | collective-permute-start | bytes 196616 | tf_op jit(solution)/shard_map/ppermute | solution.py:574
  11.3 1.3 %collective-permute-start.2 = (bf16[448,128]{1,0:T(8,128)(2,1)S(1)}, bf16[448,128]{1,0:T(8,128)(2,1)S(1)}, u32[]{:S(2)}, u32[]{:S(2)}) collective-permute-start(bf16[448,128]{1,0:T(8,128)(2,1)S(1)} %get-tuple-element.19), channel_id=1, source_target_pairs={{16,0},{17,1},{18,2},{19,3},{20,4},{21,5},{22,6},{23,7},{24,8},{25... | collective-permute-start | bytes 344072 | tf_op jit(solution)/shard_map/ppermute | solution.py:102
  12.6 2.8 %own_inner.1 = (bf16[5,1312,256]{2,1,0:T(8,128)(2,1)S(1)}, bf16[640,640]{1,0:T(8,128)(2,1)S(1)}, bf16[1360,256]{1,0:T(8,128)(2,1)S(1)}, f32[2,8,128]{2,1,0:T(8,128)S(1)}) custom-call(bf16[640,640]{1,0:T(8,128)(2,1)} %bitcast.19, bf16[1360,256]{1,0:T(8,128)(2,1)} %constant.5.clone.tables_source), custom_call_target="tpu_custom_call" | custom-call | flops 2000000000 | bytes 6000000 | tf_op jit(solution)/shard_map/own_inner/pallas_call | solution.py:609
  15.4 0.0 collective-permute-done.4.below
  15.4 0.0 copy-start
  15.4 0.0 collective-permute-done.early
  15.4 0.1 pad_maximum_fusion
  15.5 0.7 %collective-permute-start.5 = (bf16[64,128]{1,0:T(8,128)(2,1)S(1)}, bf16[64,128]{1,0:T(8,128)(2,1)S(1)}, u32[]{:S(2)}, u32[]{:S(2)}) collective-permute-start(bf16[64,128]{1,0:T(8,128)(2,1)S(1)} %pad_maximum_fusion), channel_id=1, source_target_pairs={{20,16},{24,20},{28,24},{21,17},{25,21},{29,25},{22,18},{26,22},{3... | collective-permute-start | bytes 49160 | tf_op jit(solution)/shard_map/ppermute | solution.py:590
  16.2 0.1 fusion.1
  16.3 1.9 %collective-permute-start.3 = (bf16[640,128]{1,0:T(8,128)(2,1)S(1)}, bf16[640,128]{1,0:T(8,128)(2,1)S(1)}, u32[]{:S(2)}, u32[]{:S(2)}) collective-permute-start(bf16[640,128]{1,0:T(8,128)(2,1)S(1)} %fusion.1), channel_id=1, source_target_pairs={{4,0},{8,4},{12,8},{5,1},{9,5},{13,9},{6,2},{10,6},{14,10},{7,3},{... | collective-permute-start | bytes 491528 | tf_op jit(solution)/shard_map/ppermute | solution.py:102
  18.2 0.0 collective-permute-done.1.late
  18.2 0.0 copy-done
  18.2 3.1 %shard_map.46.after_upper.left = f32[8,128]{1,0:T(8,128)S(1)} custom-call(s32[10,2,10]{2,1,0:T(2,128)S(1)} %bitcast.15, bf16[448,128]{1,0:T(8,128)(2,1)S(1)} %collective-permute-done.early, bf16[448,384]{1,0:T(8,128)(2,1)S(1)} %collective-permute-done.1.late, f32[8,128]{1,0:T(8,128)S(1)} %slice_bitcast_fusion.last.beside.left, ...), custom_call_target="tpu_custom_call" | custom-call | flops 4000000000 | bytes 6000000 | tf_op jit(solution)/shard_map/pallas_call | solution.py:613
  21.4 0.0 collective-permute-done.5.corners.beside
  21.4 1.6 %collective-permute-done.3.beside = bf16[640,128]{1,0:T(8,128)(2,1)S(1)} collective-permute-done((bf16[640,128]{1,0:T(8,128)(2,1)S(1)}, bf16[640,128]{1,0:T(8,128)(2,1)S(1)}, u32[]{:S(2)}, u32[]{:S(2)}) %collective-permute-start.3) | collective-permute-done | bytes 163872 | tf_op jit(solution)/shard_map/ppermute | solution.py:102
  22.9 0.7 %own_rest.1 = (bf16[5,1312,256]{2,1,0:T(8,128)(2,1)S(1)}, f32[2,8,128]{2,1,0:T(8,128)S(1)}) custom-call(bf16[640,640]{1,0:T(8,128)(2,1)S(1)} %get-tuple-element.22.tile, bf16[64,640]{1,0:T(8,128)(2,1)S(1)} %collective-permute-done.4.below, bf16[640,128]{1,0:T(8,128)(2,1)S(1)} %collective-permute-done.3.beside, ...), custom_call_target="tpu_custom_call", output_to_operand_aliasing={{0}: (5, {})} | custom-call | flops 2000000000 | bytes 6000000 | tf_op jit(solution)/shard_map/own_rest/pallas_call | solution.py:672
  23.6 0.0 collective-permute-done.6.last
  23.7 0.0 copy-start.1
  23.7 1.3 %collective-permute-start.7 = (f32[8,128]{1,0:T(8,128)S(1)}, f32[8,128]{1,0:T(8,128)S(1)}, u32[]{:S(2)}, u32[]{:S(2)}) collective-permute-start(f32[8,128]{1,0:T(8,128)S(1)} %shard_map.48), channel_id=1, source_target_pairs={{16,0},{17,1},{18,2},{19,3},{20,4},{21,5},{22,6},{23,7},{24,8},{25... | collective-permute-start | bytes 12296 | tf_op jit(solution)/shard_map/ppermute | solution.py:102
  25.0 0.0 collective-permute-done.2.last
  25.0 2.6 %shard_map.47.upper = f32[8,128]{1,0:T(8,128)S(1)} custom-call(s32[10,2,10]{2,1,0:T(2,128)S(1)} %bitcast.16, bf16[448,128]{1,0:T(8,128)(2,1)S(1)} %collective-permute-done.early, bf16[448,384]{1,0:T(8,128)(2,1)S(1)} %collective-permute-done.1.late, bf16[448,128]{1,0:T(8,128)(2,1)S(1)} %collective-permute-done.2.last, ...), custom_call_target="tpu_custom_call" | custom-call | flops 4000000000 | bytes 6000000 | tf_op jit(solution)/shard_map/pallas_call | solution.py:613
  27.6 4.3 %collective-permute-done.7.lower = f32[8,128]{1,0:T(8,128)S(1)} collective-permute-done((f32[8,128]{1,0:T(8,128)S(1)}, f32[8,128]{1,0:T(8,128)S(1)}, u32[]{:S(2)}, u32[]{:S(2)}) %collective-permute-start.7) | collective-permute-done | bytes 4128 | tf_op jit(solution)/shard_map/ppermute | solution.py:102
  31.9 0.0 copy-done.1
  31.9 0.7 %join.1 = f32[6,10,1,10]{3,2,1,0:T(1,128)} custom-call(f32[8,128]{1,0:T(8,128)S(1)} %shard_map.47.upper, f32[8,128]{1,0:T(8,128)S(1)} %collective-permute-done.7.lower, s32[10,1,10]{2,1,0:T(1,128)S(1)} %bitcast.17), custom_call_target="tpu_custom_call" | custom-call | tf_op jit(solution)/shard_map/join/pallas_call | solution.py:678
  (7 shorter events, 0.1 us)
Async XLA Ops:
  1.4 14.0 %collective-permute-start.4 = (bf16[64,640]{1,0:T(8,128)(2,1)S(1)}, bf16[64,640]{1,0:T(8,128)(2,1)S(1)}, u32[]{:S(2)}, u32[]{:S(2)}) collective-permute-start(bf16[64,640]{1,0:T(8,128)(2,1)S(1)} %get-tuple-element.23), channel_id=1, source_target_pairs={{17,16},{18,17},{19,18},{21,20},{22,21},{23,22},{25,24},{26,25},{2... | collective-permute-start | bytes 245768 | tf_op jit(solution)/shard_map/ppermute | solution.py:585
  2.1 13.4 %collective-permute-start = (bf16[448,128]{1,0:T(8,128)(2,1)S(1)}, bf16[448,128]{1,0:T(8,128)(2,1)S(1)}, u32[]{:S(2)}, u32[]{:S(2)}) collective-permute-start(bf16[448,128]{1,0:T(8,128)(2,1)S(1)} %get-tuple-element.17), channel_id=1, source_target_pairs={{16,0},{17,1},{18,2},{19,3},{1,16},{2,17},{3,18},{20,4},{21,5},{22... | collective-permute-start | bytes 344072 | tf_op jit(solution)/shard_map/ppermute | solution.py:576
  6.5 11.8 %collective-permute-start.1 = (bf16[448,384]{1,0:T(8,128)(2,1)S(1)}, bf16[448,384]{1,0:T(8,128)(2,1)S(1)}, u32[]{:S(2)}, u32[]{:S(2)}) collective-permute-start(bf16[448,384]{1,0:T(8,128)(2,1)S(1)} %get-tuple-element.18), channel_id=1, source_target_pairs={{0,16},{16,0},{1,17},{17,1},{2,18},{18,2},{3,19},{19,3},{4,20},{20... | collective-permute-start | bytes 1032200 | tf_op jit(solution)/shard_map/ppermute | solution.py:577
  6.7 17.0 %collective-permute-start.6 = (bf16[256,128]{1,0:T(8,128)(2,1)S(1)}, bf16[256,128]{1,0:T(8,128)(2,1)S(1)}, u32[]{:S(2)}, u32[]{:S(2)}) collective-permute-start(bf16[256,128]{1,0:T(8,128)(2,1)S(1)} %get-tuple-element.28), channel_id=1, source_target_pairs={{4,16},{8,20},{12,24},{5,17},{9,21},{13,25},{6,18},{10,22},{14,26}... | collective-permute-start | bytes 196616 | tf_op jit(solution)/shard_map/ppermute | solution.py:574
  11.3 13.7 %collective-permute-start.2 = (bf16[448,128]{1,0:T(8,128)(2,1)S(1)}, bf16[448,128]{1,0:T(8,128)(2,1)S(1)}, u32[]{:S(2)}, u32[]{:S(2)}) collective-permute-start(bf16[448,128]{1,0:T(8,128)(2,1)S(1)} %get-tuple-element.19), channel_id=1, source_target_pairs={{16,0},{17,1},{18,2},{19,3},{20,4},{21,5},{22,6},{23,7},{24,8},{25... | collective-permute-start | bytes 344072 | tf_op jit(solution)/shard_map/ppermute | solution.py:102
  15.4 2.9 %copy-start = (s32[1,2,10,10]{3,1,2,0:T(2,128)S(1)}, s32[1,2,10,10]{3,1,2,0:T(2,128)}, u32[]{:S(2)}) copy-start(s32[1,2,10,10]{3,1,2,0:T(2,128)} %param.5) | copy-start | bytes 2404
  15.5 5.8 %collective-permute-start.5 = (bf16[64,128]{1,0:T(8,128)(2,1)S(1)}, bf16[64,128]{1,0:T(8,128)(2,1)S(1)}, u32[]{:S(2)}, u32[]{:S(2)}) collective-permute-start(bf16[64,128]{1,0:T(8,128)(2,1)S(1)} %pad_maximum_fusion), channel_id=1, source_target_pairs={{20,16},{24,20},{28,24},{21,17},{25,21},{29,25},{22,18},{26,22},{3... | collective-permute-start | bytes 49160 | tf_op jit(solution)/shard_map/ppermute | solution.py:590
  16.3 6.6 %collective-permute-start.3 = (bf16[640,128]{1,0:T(8,128)(2,1)S(1)}, bf16[640,128]{1,0:T(8,128)(2,1)S(1)}, u32[]{:S(2)}, u32[]{:S(2)}) collective-permute-start(bf16[640,128]{1,0:T(8,128)(2,1)S(1)} %fusion.1), channel_id=1, source_target_pairs={{4,0},{8,4},{12,8},{5,1},{9,5},{13,9},{6,2},{10,6},{14,10},{7,3},{... | collective-permute-start | bytes 491528 | tf_op jit(solution)/shard_map/ppermute | solution.py:102
  23.7 8.3 %copy-start.1 = (s32[1,10,10]{2,0,1:T(1,128)S(1)}, s32[1,10,10]{2,0,1:T(1,128)}, u32[]{:S(2)}) copy-start(s32[1,10,10]{2,0,1:T(1,128)} %param.6) | copy-start | bytes 1204
  23.7 8.2 %collective-permute-start.7 = (f32[8,128]{1,0:T(8,128)S(1)}, f32[8,128]{1,0:T(8,128)S(1)}, u32[]{:S(2)}, u32[]{:S(2)}) collective-permute-start(f32[8,128]{1,0:T(8,128)S(1)} %shard_map.48), channel_id=1, source_target_pairs={{16,0},{17,1},{18,2},{19,3},{20,4},{21,5},{22,6},{23,7},{24,8},{25... | collective-permute-start | bytes 12296 | tf_op jit(solution)/shard_map/ppermute | solution.py:102
